TPU v7x, 512 devices: a whole 4x4x16 slice. The times are simulated.
512 devices in a mesh: samp: 64 (over z, x), blk: 8 (over y, core).
Axes of the slice: x: 4, y: 4, z: 16, core: 2. Of those that a mesh axis runs over, the one named last changes fastest.
Arguments:
- genotypes: bfloat16 [65536, 4000], P('samp', 'blk'), may hold values from 0 to 2, as said below
- traits: float32 [65536, 8], P('samp'), may hold values from -3000 to 3000
- observed: int32 [65536, 8], P('samp'), may hold values from 0 to 1, as said below
- fold_index: int32 [65536], P('samp'), may hold values from 0 to 4, never falling along the last dimension, each value on 1 to 26214 neighbouring positions
Outputs:
- stack_gram: float32 [8, 5, 40, 40], P('blk')
- stack_cross: float32 [8, 5, 40], P('blk')
Inputs may be any that keep to these rules, and one draw needn't show every extreme that they name: `genotypes`: genotype dosages, whole numbers. `observed`: each trait is measured in at least one sample.
All inputs are finite; a program needn't handle non-finite values.
Results may differ from a plain program's by a relative error of at most 0.0003.
Values sent between devices are 32-bit elements; how exact they have to be, the bound alone decides.
A program may use at most 64 MiB of HBM per device.

v0:
```python
import jax
import jax.numpy as jnp
from jax import lax
from jax.sharding import PartitionSpec as P

BLOCK = 500
TRAITS = 8
FOLDS = 5


HERITABILITY = (0.01, 0.25, 0.5, 0.75, 0.99)
PRECISE = lax.Precision.HIGHEST


def solve_one(lower_factor, right_side):
    return jax.scipy.linalg.cho_solve((lower_factor, True), right_side)


def body(genotypes, traits, observed, fold_index):
    local_rows, local_cols = genotypes.shape
    local_blocks = local_cols // BLOCK
    sample_devices = lax.axis_size("samp")
    block_devices = lax.axis_size("blk")
    samples = local_rows * sample_devices
    markers = local_cols * block_devices
    penalty_count = len(HERITABILITY)
    present = observed.astype(jnp.float32)
    masked = present * traits
    dosage_bf = genotypes.reshape(local_rows, local_blocks, BLOCK)
    dosage = dosage_bf.astype(jnp.float32)
    gram_local = jnp.einsum(
        "sbi,sbj->bij", dosage_bf, dosage_bf, preferred_element_type=jnp.float32
    )
    sums_local = jnp.sum(dosage, 0)
    trait_local = jnp.einsum("sbj,sp->bjp", dosage, masked, precision=PRECISE)
    present_local = jnp.einsum("sbj,sp->bjp", dosage, present, precision=PRECISE)
    counts_local = jnp.sum(present, 0)
    first_local = jnp.sum(masked, 0)
    second_local = jnp.sum(masked * traits, 0)
    gram_total, column_sums, dosage_trait, dosage_present, counts, trait_sums, trait_squares = (
        lax.psum(
            (
                gram_local,
                sums_local,
                trait_local,
                present_local,
                counts_local,
                first_local,
                second_local,
            ),
            "samp",
        )
    )
    mean_trait = trait_sums / counts
    trait_scale = jnp.sqrt(trait_squares / counts - mean_trait * mean_trait + 1e-05)
    scaled = present * (traits - mean_trait) / trait_scale
    mean_dosage = column_sums / samples
    dosage_scale = jnp.sqrt(
        jnp.diagonal(gram_total, axis1=1, axis2=2) / samples - mean_dosage * mean_dosage + 1e-05
    )
    covariance = (gram_total - column_sums[:, :, None] * column_sums[:, None, :] / samples) / (
        dosage_scale[:, :, None] * dosage_scale[:, None, :]
    )
    right_side = (
        (dosage_trait - dosage_present * mean_trait) / trait_scale / dosage_scale[:, :, None]
    )
    identity = jnp.eye(BLOCK, dtype=jnp.float32)
    fit_count = local_blocks * penalty_count
    position = lax.axis_index("samp")
    assigned = jnp.minimum(
        (position * fit_count + sample_devices - 1) // sample_devices, fit_count - 1
    )
    owning = assigned * sample_devices // fit_count == position
    fit_block = assigned // penalty_count
    fit_penalty = assigned % penalty_count
    penalty_table = jnp.array(
        [markers * (1.0 - fraction) / fraction for fraction in HERITABILITY], dtype=jnp.float32
    )
    penalty = jnp.sum(jnp.where(jnp.arange(penalty_count) == fit_penalty, penalty_table, 0.0))
    chosen_cov = lax.dynamic_index_in_dim(covariance, fit_block, 0, keepdims=False)
    chosen_side = lax.dynamic_index_in_dim(right_side, fit_block, 0, keepdims=False)
    lower_factor = jnp.linalg.cholesky(chosen_cov + penalty * identity)
    solution = solve_one(lower_factor, chosen_side)
    selector = jnp.logical_and(jnp.arange(fit_count) == assigned, owning).astype(jnp.float32)
    contribution = selector[:, None, None] * solution[None]
    coefficients = lax.psum(contribution, "samp").reshape(
        local_blocks, penalty_count, BLOCK, TRAITS
    )
    centred = (dosage - mean_dosage) / dosage_scale
    predicted = jnp.einsum("sbj,brjp->pbrs", centred, coefficients, precision=PRECISE)
    energy = lax.psum(jnp.sum(predicted * predicted, 3), "samp")
    standard = predicted / jnp.sqrt(energy / samples + 1e-06)[:, :, :, None]
    regrouped = lax.all_to_all(standard, "blk", split_axis=0, concat_axis=1, tiled=True)
    trait_share = TRAITS // block_devices
    stacked = regrouped.reshape(trait_share, -1, local_rows)
    first_trait = lax.axis_index("blk") * trait_share
    scaled_share = lax.dynamic_slice_in_dim(scaled, first_trait, trait_share, 1)
    present_share = lax.dynamic_slice_in_dim(present, first_trait, trait_share, 1)
    fold_hits = (fold_index[None, :] == jnp.arange(FOLDS, dtype=jnp.int32)[:, None]).astype(
        jnp.float32
    )
    weighting = fold_hits[:, None, :] * present_share.T[None]
    weighted = weighting[:, :, None, :] * stacked[None]
    gram_part = jnp.einsum("kpls,pms->pklm", weighted, stacked, precision=PRECISE)
    cross_part = jnp.einsum("kpls,sp->pkl", weighted, scaled_share, precision=PRECISE)
    gram_sum, cross_sum = lax.psum((gram_part, cross_part), "samp")
    factor = FOLDS / samples
    return (gram_sum * factor, cross_sum * factor)


def solution(mesh):
    in_specs = (P("samp", "blk"), P("samp", None), P("samp", None), P("samp"))
    out_specs = (P("blk", None, None, None), P("blk", None, None))
    return jax.shard_map(body, mesh=mesh, in_specs=in_specs, out_specs=out_specs, check_vma=False)
```

profile of v0, /device:TPU:8, one launch (start us, length us, event | category | flops | bytes accessed | tf_op | source)
XLA Modules:
  0.0 1162.0 jit_solution(14717013578681250181)
XLA Ops:
  7.2 3.3 convolution_bitcast_fusion
  10.6 1.1 copy-done.1
  12.0 0.9 convolution_bitcast_fusion.1
  14.6 285.7 %all-reduce.4 = (f32[1,500]{1,0:T(1,128)S(1)}, f32[1,500,8]{1,2,0:T(8,128)}, f32[1,500,8]{1,2,0:T(8,128)}, f32[8]{0:T(128)S(1)}, f32[8]{0:T(128)S(1)}, /*index=5*/f32[8]{0:T(128)S(1)}) all-reduce(f32[1,500]{1,0:T(1,128)S(1)} %bitcast.135, f32[1,500,8]{1,2,0:T(8,128)S(1)} %convolution_bitcast_fusion.2, ...), channel_id=1, replica_groups=mesh['samp'=64,'blk'=8] {'samp'}, use_global_device_ids=true, to_apply=%region_2.0 | all-reduce | flops 8524 | bytes 68192 | tf_op jit(solution)/shard_map/psum | solution.py:41
  303.8 10.4 gather_fusion
  314.8 1.9 bitcast_add_fusion.1
  316.7 1.5 copy.16
  318.3 1.0 fusion.14
  319.3 1.0 copy-done.2
  320.3 11.7 %cholesky.104 = f32[128,128]{1,0:T(8,128)S(1)} custom-call(f32[128,128]{1,0:T(8,128)S(1)} %cholesky.269), custom_call_target="Cholesky" | custom-call | tf_op jit(solution)/shard_map/jit(cholesky)/cholesky | solution.py:82
  332.8 9.8 custom-call.34
  344.2 13.2 %cholesky.217 = f32[128,128]{1,0:T(8,128)} custom-call(f32[128,128]{1,0:T(8,128)} %cholesky.273), custom_call_target="Cholesky" | custom-call | tf_op jit(solution)/shard_map/jit(cholesky)/cholesky | solution.py:82
  357.4 2.0 select_reduce_fusion.1
  359.4 11.4 custom-call.35
  370.8 1.2 convolution_dynamic-update-slice_fusion
  372.4 12.3 %cholesky.238 = f32[128,128]{1,0:T(8,128)} custom-call(f32[128,128]{1,0:T(8,128)S(1)} %cholesky.278), custom_call_target="Cholesky" | custom-call | tf_op jit(solution)/shard_map/jit(cholesky)/cholesky | solution.py:82
  386.3 10.4 custom-call.36
  396.8 1.1 convolution_dynamic-update-slice_fusion.1
  398.2 10.8 cholesky.258
  409.7 1.3 compare_reduce_fusion.2
  414.2 6.3 while.1
  414.9 1.4 bitcast_dynamic-update-slice_fusion.2
  417.0 1.4 bitcast_dynamic-update-slice_fusion.2
  419.2 1.4 bitcast_dynamic-update-slice_fusion.2
  420.7 39.3 %custom-call.37 = f32[4,128,128]{1,2,0:T(8,128)S(1)} custom-call(f32[4,128,128]{2,1,0:T(8,128)S(1)} %pad_maximum_fusion), custom_call_target="InvertDiagBlocksLowerTriangular" | custom-call | tf_op jit(solution)/shard_map/jit(_cho_solve)/triangular_solve | solution.py:16
  464.7 257.0 %all-reduce.10.cloned.1.call-done = f32[5,500,8]{1,2,0:T(8,128)} async-done(((f32[5,500,8]{1,2,0:T(8,128)}), f32[5,500,8]{1,2,0:T(8,128)}) %all-reduce.10.cloned.1.call-update) | async-done | bytes 80016 | tf_op jit(solution)/shard_map/psum | solution.py:86
  721.7 2.5 multiply_reduce_fusion
  724.3 139.6 %psum.88 = f32[8,1,5]{2,0,1:T(8,128)S(1)} all-reduce(f32[8,1,5]{2,0,1:T(8,128)S(1)} %bitcast.133), channel_id=1, replica_groups=mesh['samp'=64,'blk'=8] {'samp'}, use_global_device_ids=true, to_apply=%region_22.23 | all-reduce | flops 40 | bytes 320 | tf_op jit(solution)/shard_map/psum | solution.py:91
  865.0 4.8 all-to-all-start
  869.8 5.0 all-to-all-done
  875.3 3.2 fusion.4
  879.3 274.3 %all-reduce.3 = (f32[1,5,40,40]{3,2,1,0:T(8,128)S(1)}, f32[1,5,40]{2,0,1:T(1,128)S(1)}) all-reduce(f32[1,5,40,40]{3,2,1,0:T(8,128)S(1)} %fusion.11, f32[1,5,40]{2,0,1:T(1,128)S(1)} %dot_general.44), channel_id=1, replica_groups=mesh['samp'=64,'blk'=8] {'samp'}, use_global_device_ids=true, to_apply=%region_23.24 | all-reduce | flops 8200 | bytes 65600 | tf_op jit(solution)/shard_map/psum | solution.py:106
  (109 shorter events, 22.3 us)
Async XLA Ops:
  7.2 296.6 %all-reduce.8.cloned.1.call-start = ((), (), s32[]{:S(2)}) async-start(), calls=%async_computation.1 | async-start | bytes 2064384 | tf_op jit(solution)/shard_map/psum | solution.py:41
  10.5 1.2 copy-start.1
  10.5 1.5 copy-start.4
  10.5 711.2 %all-reduce.10.cloned.1.call-start = ((), (), s32[]{:S(2)}) async-start(), calls=%async_computation.2 | async-start | bytes 163840 | tf_op jit(solution)/shard_map/psum | solution.py:86
  11.7 1.8 copy-start.5
  12.0 291.2 %copy-start.15 = (f32[5]{0:T(128)S(1)}, f32[5]{0:T(128)}, u32[]{:S(2)}) copy-start(f32[5]{0:T(128)} %constant.250.clone) | copy-start | bytes 64
  300.3 0.6 copy-start.11
  300.3 1.1 copy-start.9
  303.8 11.0 copy-start
  319.3 1.0 copy-start.2
  320.3 22.3 %copy-start.3 = (f32[500,500]{1,0:T(8,128)S(1)}, f32[500,500]{1,0:T(8,128)}, u32[]{:S(2)}) copy-start(f32[500,500]{1,0:T(8,128)} %copy-done.2) | copy-start | bytes 3000004
  413.6 0.7 copy-start.16
  413.7 46.3 %copy-start.6 = (f32[1,500,8]{1,2,0:T(8,128)S(1)}, f32[1,500,8]{1,2,0:T(8,128)}, u32[]{:S(2)}) copy-start(f32[1,500,8]{1,2,0:T(8,128)} %get-tuple-element.24) | copy-start | bytes 48004
  413.7 46.3 %copy-start.7 = (f32[1,500,8]{1,2,0:T(8,128)S(1)}, f32[1,500,8]{1,2,0:T(8,128)}, u32[]{:S(2)}) copy-start(f32[1,500,8]{1,2,0:T(8,128)} %get-tuple-element.25) | copy-start | bytes 48004
  413.7 46.3 %copy-start.10 = (f32[8]{0:T(128)S(1)}, f32[8]{0:T(128)}, u32[]{:S(2)}) copy-start(f32[8]{0:T(128)} %copy-done.9) | copy-start | bytes 100
  413.7 46.3 %copy-start.12 = (f32[8]{0:T(128)S(1)}, f32[8]{0:T(128)}, u32[]{:S(2)}) copy-start(f32[8]{0:T(128)} %copy-done.11) | copy-start | bytes 100
  420.7 42.5 %copy-start.14 = (f32[5]{0:T(128)S(1)}, f32[5]{0:T(128)}, u32[]{:S(2)}) copy-start(f32[5]{0:T(128)} %and_convert_fusion) | copy-start | bytes 64
  420.7 301.0 %copy-start.13 = (f32[1,500]{1,0:T(1,128)S(1)}, f32[1,500]{1,0:T(1,128)}, u32[]{:S(2)}) copy-start(f32[1,500]{1,0:T(1,128)} %get-tuple-element.43) | copy-start | bytes 6004
  721.7 148.1 %copy-start.8 = (s32[1024]{0:T(1024)S(1)}, s32[1024]{0:T(1024)}, u32[]{:S(2)}) copy-start(s32[1024]{0:T(1024)} %param.8) | copy-start | bytes 12292
  865.0 9.8 all-to-all-start
Sparse Core Ops, SparseCore 0:
  11.4 280.3 all-reduce.7
  464.0 257.6 all-reduce.9
where the time goes:
time: 1170 us; the launch traced here: 1160 us
  blocking collectives  700 us (60%)
  waiting for transfers between devices  262 us (22%)
  other arithmetic  134 us (11%)
  local copies, waits for them, and re-layouts  25.2 us (2%)
  matrix products  18.5 us (2%)
  between operations  17.3 us (1%)
    psum x1, blocking collectives, body(): lax.psum((gram_local, sums_local, trait_local, present_local, counts_loca...  286 us
    psum x1, blocking collectives, body(): gram_sum, cross_sum = lax.psum((gram_part, cross_part), 'samp')  274 us
    psum x1, waiting for transfers between devices, body(): lax.psum(contribution, 'samp')  257 us
    psum x1, blocking collectives, body(): energy = lax.psum(jnp.sum(predicted * predicted, 3), 'samp')  140 us
    another operation x14, other arithmetic, body(): lower_factor = jnp.linalg.cholesky(chosen_cov + penalty * identity)  85.9 us
    another operation x8, other arithmetic, solve_one(): return jax.scipy.linalg.cho_solve((lower_factor, True), right_side)  40.2 us
  transfers between devices with their start and end apart: 3, of which 2 were waited for; matrix products, arithmetic and copies ran while one was open for 1% of the time, Pallas kernels for 0%

commit v1 on v0

v1 whole, which is shorter than its diff:
```python
import functools

import jax
import jax.numpy as jnp
from jax import lax
from jax.experimental import pallas as pl
from jax.experimental.pallas import tpu as pltpu
from jax.sharding import PartitionSpec as P

BLOCK = 500
TRAITS = 8
FOLDS = 5
HERITABILITY = (0.01, 0.25, 0.5, 0.75, 0.99)
PENALTIES = len(HERITABILITY)
PRECISE = lax.Precision.HIGHEST
MESH = pl.DeviceIdType.MESH

XS = 4
LANES = 128
TILES = 4
WIDTH = TILES * LANES
ONES = BLOCK
PAIRS = [(i, j) for i in range(TILES) for j in range(i, TILES)]
EXTRA = 24
FLAT = len(PAIRS) * LANES + TILES * EXTRA
QUARTER = FLAT // XS
HALF = 176
STACK = PENALTIES * 8


def pieces(start, rows):
    out = []
    while rows > 0:
        quarter, row = divmod(start, QUARTER)
        take = min(rows, QUARTER - row)
        out.append((quarter, row, take))
        start += take
        rows -= take
    return out


def put(ref, start, value):
    done = 0
    for quarter, row, take in pieces(start, value.shape[0]):
        ref[quarter, row : row + take, :] = value[done : done + take]
        done += take


def get(ref, start, rows):
    parts = [ref[quarter, row : row + take, :] for quarter, row, take in pieces(start, rows)]
    return parts[0] if len(parts) == 1 else jnp.concatenate(parts, axis=0)


def split3(value):
    first = value.astype(jnp.bfloat16).astype(jnp.float32)
    rest = value - first
    second = rest.astype(jnp.bfloat16).astype(jnp.float32)
    third = rest - second
    return first, second, third


def remote(src, dst, send, recv, samp, blk):
    return pltpu.make_async_remote_copy(
        src_ref=src,
        dst_ref=dst,
        send_sem=send,
        recv_sem=recv,
        device_id=(samp, blk),
        device_id_type=MESH,
    )


def gram_kernel(
    zs, chunk, g_ref, aux_ref, out_ref, g_scr, pay, from_left, from_right, acc, z_in, mine, z_all,
    total, xs_send, xs_recv, zr_send, zr_recv, zg_send, zg_recv, xg_send, xg_recv,
):
    samp = lax.axis_index("samp")
    blk = lax.axis_index("blk")
    z = samp // XS
    x = lax.rem(samp, XS)
    right = lax.rem(x + 1, XS)
    left = lax.rem(x + XS - 1, XS)
    far = lax.rem(x + 2, XS)
    to_right = z * XS + right
    to_left = z * XS + left

    barrier = pltpu.get_barrier_semaphore()
    for side in (to_right, to_left):
        pl.semaphore_signal(barrier, inc=1, device_id=(side, blk), device_id_type=MESH)

    def greet(i, carry):
        other = lax.rem(z + i + 1, zs) * XS + x
        pl.semaphore_signal(barrier, inc=1, device_id=(other, blk), device_id_type=MESH)
        return carry

    lax.fori_loop(0, zs - 1, greet, 0)

    rows = g_ref.shape[0]
    tail = lax.broadcasted_iota(jnp.int32, (rows, LANES), 1) == ONES - (TILES - 1) * LANES
    g_scr[:, (TILES - 1) * LANES :] = tail.astype(jnp.float32).astype(jnp.bfloat16)
    g_scr[:, :BLOCK] = g_ref[...]
    traits = aux_ref[0:8, :]
    present = aux_ref[8:16, :]
    masked = traits * present
    squares = jnp.sum(masked * traits, axis=1, keepdims=True)
    ones = (lax.broadcasted_iota(jnp.int32, masked.shape, 0) == 0).astype(jnp.float32)
    stacked = jnp.concatenate([*split3(masked), present, ones], axis=0).astype(jnp.bfloat16)
    products = jnp.dot(stacked, g_scr[...], preferred_element_type=jnp.float32)
    for j in range(TILES):
        cols = products[:, j * LANES : (j + 1) * LANES]
        last = cols[32:40]
        if j == TILES - 1:
            lane = lax.broadcasted_iota(jnp.int32, last.shape, 1)
            last = jnp.where(lane == ONES + 1 - j * LANES, squares, last)
        base = len(PAIRS) * LANES + j * EXTRA
        put(pay, base, cols[0:8] + (cols[8:16] + cols[16:24]))
        put(pay, base + 8, cols[24:32])
        put(pay, base + 16, last)
    slot = 0
    for i in range(TILES):
        strip = lax.dot_general(
            g_scr[:, i * LANES : (i + 1) * LANES],
            g_scr[:, i * LANES :],
            (((0,), (0,)), ((), ())),
            preferred_element_type=jnp.float32,
        )
        for j in range(i, TILES):
            put(pay, slot * LANES, strip[:, (j - i) * LANES : (j - i + 1) * LANES])
            slot += 1
    acc[QUARTER:, :] = jnp.zeros((acc.shape[0] - QUARTER, LANES), jnp.float32)

    pl.semaphore_wait(barrier, 2 + zs - 1)

    first = pl.ds(0, HALF)
    second = pl.ds(HALF, QUARTER - HALF)
    a1 = remote(pay.at[far, first], from_left.at[0, first], xs_send.at[0], xs_recv.at[0], to_right, blk)
    a2 = remote(pay.at[far, second], from_right.at[0, second], xs_send.at[1], xs_recv.at[1], to_left, blk)
    a3 = remote(pay.at[right, second], from_left.at[1, second], xs_send.at[2], xs_recv.at[2], to_right, blk)
    a4 = remote(pay.at[left, first], from_right.at[1, first], xs_send.at[3], xs_recv.at[3], to_left, blk)
    a5 = remote(pay.at[right, first], from_left.at[1, first], xs_send.at[4], xs_recv.at[4], to_right, blk)
    a6 = remote(pay.at[left, second], from_right.at[1, second], xs_send.at[5], xs_recv.at[5], to_left, blk)
    a1.start()
    a2.start()
    a3.start()
    a4.start()
    a1.wait_recv()
    pay[right, 0:HALF, :] = pay[right, 0:HALF, :] + from_left[0, 0:HALF, :]
    a5.start()
    a2.wait_recv()
    pay[left, HALF:QUARTER, :] = pay[left, HALF:QUARTER, :] + from_right[0, HALF:QUARTER, :]
    a6.start()
    for copy in (a3, a4, a5, a6):
        copy.wait_recv()
    acc[0:QUARTER, :] = pay[x, 0:QUARTER, :] + (from_left[1, 0:QUARTER, :] + from_right[1, 0:QUARTER, :])

    def scatter(i):
        other = lax.rem(z + i + 1, zs)
        rows_there = pl.ds(pl.multiple_of(other * chunk, 8), chunk)
        return remote(acc.at[rows_there], z_in.at[i], zr_send.at[i], zr_recv.at[i], other * XS + x, blk)

    def start_scatter(i, carry):
        scatter(i).start()
        return carry

    def wait_scatter(i, carry):
        scatter(i).wait_recv()
        return carry

    lax.fori_loop(0, zs - 1, start_scatter, 0)
    lax.fori_loop(0, zs - 1, wait_scatter, 0)
    here = acc[pl.ds(pl.multiple_of(z * chunk, 8), chunk), :]
    for i in range(zs - 1):
        here = here + z_in[i]
    mine[...] = here
    mine_rows = pl.ds(pl.multiple_of(z * chunk, 8), chunk)
    z_all[mine_rows, :] = here

    def gather(i):
        other = lax.rem(z + i + 1, zs)
        return remote(mine, z_all.at[mine_rows], zg_send.at[i], zg_recv.at[i], other * XS + x, blk)

    def start_gather(i, carry):
        gather(i).start()
        return carry

    def wait_gather(i, carry):
        gather(i).wait_recv()
        return carry

    lax.fori_loop(0, zs - 1, start_gather, 0)
    lax.fori_loop(0, zs - 1, wait_gather, 0)

    quarter = pl.ds(0, QUARTER)
    b1 = remote(z_all.at[quarter], total.at[x, quarter], xg_send.at[0], xg_recv.at[0], to_right, blk)
    b2 = remote(z_all.at[quarter], total.at[x, quarter], xg_send.at[1], xg_recv.at[1], to_left, blk)
    b3 = remote(total.at[left, first], total.at[left, first], xg_send.at[2], xg_recv.at[2], to_right, blk)
    b4 = remote(total.at[right, second], total.at[right, second], xg_send.at[3], xg_recv.at[3], to_left, blk)
    b1.start()
    b2.start()
    total[x, 0:QUARTER, :] = z_all[0:QUARTER, :]
    b1.wait_recv()
    b3.start()
    b2.wait_recv()
    b4.start()
    b3.wait_recv()
    b4.wait_recv()
    out_ref[...] = total[...]

    for copy in (a1, a2, a3, a4, a5, a6, b1, b2, b3, b4):
        copy.wait_send()

    def drain(i, carry):
        scatter(i).wait_send()
        gather(i).wait_send()
        return carry

    lax.fori_loop(0, zs - 1, drain, 0)


def sum_grams(genotypes, aux, zs):
    chunk = -(-QUARTER // (8 * zs)) * 8
    rows = genotypes.shape[0]
    vmem = pl.BlockSpec(memory_space=pltpu.VMEM)
    dma = pltpu.SemaphoreType.DMA
    return pl.pallas_call(
        functools.partial(gram_kernel, zs, chunk),
        out_shape=jax.ShapeDtypeStruct((XS, QUARTER, LANES), jnp.float32),
        in_specs=[vmem, vmem],
        out_specs=vmem,
        scratch_shapes=[
            pltpu.VMEM((rows, WIDTH), jnp.bfloat16),
            pltpu.VMEM((XS, QUARTER, LANES), jnp.float32),
            pltpu.VMEM((2, QUARTER, LANES), jnp.float32),
            pltpu.VMEM((2, QUARTER, LANES), jnp.float32),
            pltpu.VMEM((zs * chunk, LANES), jnp.float32),
            pltpu.VMEM((zs - 1, chunk, LANES), jnp.float32),
            pltpu.VMEM((chunk, LANES), jnp.float32),
            pltpu.VMEM((zs * chunk, LANES), jnp.float32),
            pltpu.VMEM((XS, QUARTER, LANES), jnp.float32),
            dma((6,)),
            dma((6,)),
            dma((zs - 1,)),
            dma((zs - 1,)),
            dma((zs - 1,)),
            dma((zs - 1,)),
            dma((4,)),
            dma((4,)),
        ],
        compiler_params=pltpu.CompilerParams(
            collective_id=0, has_side_effects=True, vmem_limit_bytes=48 << 20
        ),
        name="sum_grams",
    )(genotypes, aux)


def invert(a_ref):
    lane = lax.broadcasted_iota(jnp.int32, (8, LANES), 1)
    sub = lax.broadcasted_iota(jnp.int32, (8, LANES), 0)
    wide = lax.broadcasted_iota(jnp.int32, (LANES, LANES), 1)

    def panel(q, carry):
        base = pl.multiple_of(q * 8, 8)
        shift = lax.rem(LANES - base, LANES)
        strip = a_ref[pl.ds(base, 8), :]
        turned = pltpu.roll(strip, shift, 1)
        cols = [jnp.broadcast_to(turned[:, j : j + 1], (8, LANES)) for j in range(8)]
        inside = jnp.logical_and(lane >= base, lane < base + 8)
        solved = jnp.where(inside, jnp.where(lane - base == sub, -1.0, 0.0), strip)
        for j in range(8):
            inverse = 1.0 / cols[j][j : j + 1, :]
            row = solved[j : j + 1, :] * inverse
            solved = jnp.where(sub == j, row, solved - cols[j] * row)
            for m in range(j + 1, 8):
                value = cols[m][j : j + 1, :] * inverse
                cols[m] = jnp.where(sub == j, value, cols[m] - cols[j] * value)
        whole = a_ref[...]
        turned_all = pltpu.roll(whole, shift, 1)
        within = jnp.logical_and(wide >= base, wide < base + 8)
        result = jnp.where(within, 0.0, whole)
        for j in range(8):
            result = result - turned_all[:, j : j + 1] * solved[j : j + 1, :]
        a_ref[...] = result
        a_ref[pl.ds(base, 8), :] = solved
        return carry

    lax.fori_loop(0, LANES // 8, panel, 0)


def solve_kernel(samples, markers, total_ref, beta_ref, stat_ref, cov, work, inv):
    samp = lax.axis_index("samp")
    place = lax.rem(samp, 2 * XS)
    weight = jnp.float32(0.0)
    for r, fraction in enumerate(HERITABILITY):
        value = jnp.float32(markers * (1.0 - fraction) / fraction)
        chosen = place == r if r < PENALTIES - 1 else place >= r
        weight = jnp.where(chosen, value, weight)

    dot = functools.partial(jnp.dot, precision=PRECISE, preferred_element_type=jnp.float32)

    def dot_t(a, b):
        return lax.dot_general(
            a, b, (((0,), (0,)), ((), ())), precision=PRECISE, preferred_element_type=jnp.float32
        )

    def dot_nt(a, b):
        return lax.dot_general(
            a, b, (((1,), (1,)), ((), ())), precision=PRECISE, preferred_element_type=jnp.float32
        )

    slot = {pair: n for n, pair in enumerate(PAIRS)}
    gram = {pair: get(total_ref, n * LANES, LANES) for pair, n in slot.items()}
    extra = [get(total_ref, len(PAIRS) * LANES + j * EXTRA, EXTRA) for j in range(TILES)]
    eye = lax.broadcasted_iota(jnp.int32, (LANES, LANES), 0) == lax.broadcasted_iota(
        jnp.int32, (LANES, LANES), 1
    )
    mark = ONES - (TILES - 1) * LANES
    sums = extra[-1][0:8, mark : mark + 1]
    counts = extra[-1][8:16, mark : mark + 1]
    squares = extra[-1][16:24, mark + 1 : mark + 2]
    mean_trait = sums / counts
    trait_scale = jnp.sqrt(squares / counts - mean_trait * mean_trait + 1e-05)
    lane8 = lax.broadcasted_iota(jnp.int32, (8, LANES), 1)
    stat_ref[...] = jnp.where(lane8 == 0, mean_trait, jnp.where(lane8 == 1, trait_scale, 0.0))

    sum_row, mean_row, scale_row, sum_col, scale_col = [], [], [], [], []
    for j in range(TILES):
        diagonal = jnp.where(eye, gram[(j, j)], 0.0)
        row = extra[j][16:17, :]
        if j == TILES - 1:
            row = jnp.where(lane8[0:1] < mark, row, 0.0)
        col = gram[(j, TILES - 1)][:, mark : mark + 1]
        mean = row / samples
        mean_c = col / samples
        sum_row.append(row)
        mean_row.append(mean)
        sum_col.append(col)
        squares_row = jnp.sum(diagonal, axis=0, keepdims=True)
        squares_col = jnp.sum(diagonal, axis=1, keepdims=True)
        scale_row.append(jnp.sqrt(squares_row / samples - mean * mean + 1e-05))
        scale_col.append(jnp.sqrt(squares_col / samples - mean_c * mean_c + 1e-05))
    lane = lax.broadcasted_iota(jnp.int32, (LANES, LANES), 1)
    sub = lax.broadcasted_iota(jnp.int32, (LANES, LANES), 0)
    for (i, j), n in slot.items():
        value = (gram[(i, j)] - sum_col[i] * sum_row[j] / samples) / (scale_col[i] * scale_row[j])
        if j == TILES - 1:
            value = jnp.where(lane < mark, value, 0.0)
        if i == TILES - 1:
            value = jnp.where(sub < mark, value, 0.0)
        cov[n] = value
        work[n] = jnp.where(eye, value + weight, value) if i == j else value
    side = []
    for j in range(TILES):
        value = (extra[j][0:8] - extra[j][8:16] * mean_trait) / trait_scale / scale_row[j]
        if j == TILES - 1:
            value = jnp.where(lane8 < mark, value, 0.0)
        side.append(value)

    for k in range(TILES):
        a_ref = inv.at[k]
        a_ref[...] = work[slot[(k, k)]]
        invert(a_ref)
        minus = inv[k]
        for j in range(k + 1, TILES):
            ahead = dot(minus, work[slot[(k, j)]])
            for i in range(k + 1, j + 1):
                n = slot[(i, j)]
                work[n] = work[n] + dot_t(work[slot[(k, i)]], ahead)
        if k < TILES - 1:
            part = dot(side[k], minus)
            for j in range(k + 1, TILES):
                side[j] = side[j] + dot(part, work[slot[(k, j)]])

    found = [None] * TILES
    for k in range(TILES - 1, -1, -1):
        value = side[k]
        for j in range(k + 1, TILES):
            value = value - dot_nt(found[j], work[slot[(k, j)]])
        found[k] = -dot(value, inv[k])

    energy = jnp.zeros((8, 1), jnp.float32)
    shift = jnp.zeros((8, 1), jnp.float32)
    betas = []
    for k in range(TILES):
        image = dot(found[k], cov[slot[(k, k)]])
        for j in range(k + 1, TILES):
            image = image + 2.0 * dot_nt(found[j], cov[slot[(k, j)]])
        energy = energy + jnp.sum(image * found[k], axis=1, keepdims=True)
        beta = found[k] / scale_row[k]
        shift = shift + jnp.sum(beta * mean_row[k], axis=1, keepdims=True)
        betas.append(beta)
    norm = 1.0 / jnp.sqrt(energy / samples + 1e-06)
    for k in range(TILES):
        value = betas[k]
        if k == TILES - 1:
            value = jnp.where(lane8 == mark, -shift, jnp.where(lane8 < mark, value, 0.0))
        beta_ref[:, k * LANES : (k + 1) * LANES] = value * norm


def solve(total, samples, markers):
    vmem = pl.BlockSpec(memory_space=pltpu.VMEM)
    return pl.pallas_call(
        functools.partial(solve_kernel, samples, markers),
        out_shape=(
            jax.ShapeDtypeStruct((8, WIDTH), jnp.float32),
            jax.ShapeDtypeStruct((8, LANES), jnp.float32),
        ),
        in_specs=[vmem],
        out_specs=(vmem, vmem),
        scratch_shapes=[
            pltpu.VMEM((len(PAIRS), LANES, LANES), jnp.float32),
            pltpu.VMEM((len(PAIRS), LANES, LANES), jnp.float32),
            pltpu.VMEM((TILES, LANES, LANES), jnp.float32),
        ],
        compiler_params=pltpu.CompilerParams(vmem_limit_bytes=48 << 20),
        name="solve",
    )(total)


def share_kernel(beta_ref, out_ref, held, send, recv):
    samp = lax.axis_index("samp")
    blk = lax.axis_index("blk")
    group = 2 * XS
    place = lax.rem(samp, group)
    first = samp - place
    barrier = pltpu.get_barrier_semaphore()
    for i in range(group - 1):
        other = first + lax.rem(place + i + 1, group)
        pl.semaphore_signal(barrier, inc=1, device_id=(other, blk), device_id_type=MESH)
    pl.semaphore_wait(barrier, group - 1)

    def copy(i):
        other = first + lax.rem(place + i + 1, group)
        return remote(beta_ref, held.at[place], send.at[i], recv.at[place], other, blk)

    @pl.when(place < PENALTIES)
    def _():
        for i in range(group - 1):
            copy(i).start()
        held[place] = beta_ref[...]

    for r in range(PENALTIES):

        @pl.when(place != r)
        def _():
            pltpu.make_async_copy(held.at[r], held.at[r], recv.at[r]).wait()

    out_ref[...] = jnp.zeros_like(out_ref)
    for r in range(PENALTIES):
        out_ref[:, r, :] = held[r]

    @pl.when(place < PENALTIES)
    def _():
        for i in range(group - 1):
            copy(i).wait_send()


def share(beta):
    vmem = pl.BlockSpec(memory_space=pltpu.VMEM)
    return pl.pallas_call(
        share_kernel,
        out_shape=jax.ShapeDtypeStruct((TRAITS, 8, WIDTH), jnp.float32),
        in_specs=[vmem],
        out_specs=vmem,
        scratch_shapes=[
            pltpu.VMEM((PENALTIES, 8, WIDTH), jnp.float32),
            pltpu.SemaphoreType.DMA((2 * XS - 1,)),
            pltpu.SemaphoreType.DMA((PENALTIES,)),
        ],
        compiler_params=pltpu.CompilerParams(collective_id=1, has_side_effects=True),
        name="share",
    )(beta)


PARTS = 24


def stack_kernel(
    zs, factor, g_ref, aux_ref, beta_ref, stat_ref, out_ref, g_scr, outgoing, incoming, columns,
    weights, part, x_in, z_all, mine, total, a_send, a_recv, xs_send, xs_recv, z_send, z_recv,
    xg_send, xg_recv,
):
    samp = lax.axis_index("samp")
    blk = lax.axis_index("blk")
    z = samp // XS
    x = lax.rem(samp, XS)
    barrier = pltpu.get_barrier_semaphore()

    def trait_peer(i):
        return lax.rem(blk + i + 1, TRAITS)

    def x_peer(i):
        return z * XS + lax.rem(x + i + 1, XS)

    def z_peer(i):
        return lax.rem(z + i + 1, zs) * XS + x

    for i in range(TRAITS - 1):
        pl.semaphore_signal(barrier, inc=1, device_id=(samp, trait_peer(i)), device_id_type=MESH)
    for i in range(XS - 1):
        pl.semaphore_signal(barrier, inc=1, device_id=(x_peer(i), blk), device_id_type=MESH)

    def greet(i, carry):
        pl.semaphore_signal(barrier, inc=1, device_id=(z_peer(i), blk), device_id_type=MESH)
        return carry

    lax.fori_loop(0, zs - 1, greet, 0)

    rows = g_ref.shape[0]
    tail = lax.broadcasted_iota(jnp.int32, (rows, LANES), 1) == ONES - (TILES - 1) * LANES
    g_scr[:, (TILES - 1) * LANES :] = tail.astype(jnp.float32).astype(jnp.bfloat16)
    g_scr[:, :BLOCK] = g_ref[...]
    beta = beta_ref[...].reshape(TRAITS * 8, WIDTH)
    stacked = jnp.concatenate(split3(beta), axis=0).astype(jnp.bfloat16)
    predicted = lax.dot_general(
        stacked, g_scr[...], (((1,), (1,)), ((), ())), preferred_element_type=jnp.float32
    )
    n = TRAITS * 8
    predicted = predicted[0:n] + (predicted[n : 2 * n] + predicted[2 * n :])
    outgoing[...] = predicted.reshape(TRAITS, 8, rows)

    which = lax.broadcasted_iota(jnp.int32, (8, rows), 0) == blk
    present = jnp.sum(jnp.where(which, aux_ref[8:16, :], 0.0), axis=0, keepdims=True)
    mean = stat_ref[:, 0:1]
    scale = stat_ref[:, 1:2]
    scaled_all = aux_ref[8:16, :] * (aux_ref[0:8, :] - mean) / scale
    scaled = jnp.sum(jnp.where(which, scaled_all, 0.0), axis=0, keepdims=True)
    fold = aux_ref[16:17, :]

    pl.semaphore_wait(barrier, TRAITS - 1 + XS - 1 + zs - 1)

    def exchange(i):
        other = trait_peer(i)
        return remote(outgoing.at[other], incoming.at[blk], a_send.at[i], a_recv.at[i], samp, other)

    for i in range(TRAITS - 1):
        exchange(i).start()
    incoming[blk] = outgoing[blk]
    for i in range(TRAITS - 1):
        exchange(i).wait_recv()

    for b in range(TRAITS):
        columns[b * PENALTIES : (b + 1) * PENALTIES, :] = incoming[b, 0:PENALTIES, :]
    stacked_cols = columns[...]
    for k in range(FOLDS):
        hit = jnp.where(fold == float(k), present, 0.0)
        weights[k * STACK : (k + 1) * STACK, :] = stacked_cols * hit
    end = FOLDS * STACK
    picked = lax.broadcasted_iota(jnp.int32, (8, rows), 0).astype(jnp.float32) == fold
    weights[end : end + 8, :] = jnp.where(picked, scaled, 0.0)
    weights[end + 8 :, :] = jnp.zeros((weights.shape[0] - end - 8, rows), jnp.float32)
    local = lax.dot_general(
        stacked_cols,
        weights[...],
        (((1,), (1,)), ((), ())),
        precision=PRECISE,
        preferred_element_type=jnp.float32,
    )
    flat = jnp.concatenate(
        [
            local[:, 0:LANES],
            local[:, LANES:],
            jnp.zeros((XS * PARTS - 2 * STACK, LANES), jnp.float32),
        ],
        axis=0,
    )
    for q in range(XS):
        part[q] = flat[q * PARTS : (q + 1) * PARTS]

    def scatter(i):
        there = lax.rem(x + i + 1, XS)
        return remote(part.at[there], x_in.at[i], xs_send.at[i], xs_recv.at[i], x_peer(i), blk)

    for i in range(XS - 1):
        scatter(i).start()
    for i in range(XS - 1):
        scatter(i).wait_recv()
    value = part[x] + (x_in[0] + (x_in[1] + x_in[2]))
    mine[...] = value
    z_all[z] = value

    def spread(i):
        return remote(mine, z_all.at[z], z_send.at[i], z_recv.at[i], z_peer(i), blk)

    def start_spread(i, carry):
        spread(i).start()
        return carry

    def wait_spread(i, carry):
        spread(i).wait_recv()
        return carry

    lax.fori_loop(0, zs - 1, start_spread, 0)
    lax.fori_loop(0, zs - 1, wait_spread, 0)
    value = z_all[0]
    for i in range(1, zs):
        value = value + z_all[i]
    total[x] = value * factor

    def collect(i):
        return remote(total.at[x], total.at[x], xg_send.at[i], xg_recv.at[i], x_peer(i), blk)

    for i in range(XS - 1):
        collect(i).start()
    for i in range(XS - 1):
        collect(i).wait_recv()
    out_ref[...] = total[...]

    for i in range(TRAITS - 1):
        exchange(i).wait_send()
    for i in range(XS - 1):
        scatter(i).wait_send()
        collect(i).wait_send()

    def drain(i, carry):
        spread(i).wait_send()
        return carry

    lax.fori_loop(0, zs - 1, drain, 0)


def stack(genotypes, aux, betas, stats, zs, factor):
    rows = genotypes.shape[0]
    vmem = pl.BlockSpec(memory_space=pltpu.VMEM)
    dma = pltpu.SemaphoreType.DMA
    return pl.pallas_call(
        functools.partial(stack_kernel, zs, factor),
        out_shape=jax.ShapeDtypeStruct((XS, PARTS, LANES), jnp.float32),
        in_specs=[vmem] * 4,
        out_specs=vmem,
        scratch_shapes=[
            pltpu.VMEM((rows, WIDTH), jnp.bfloat16),
            pltpu.VMEM((TRAITS, 8, rows), jnp.float32),
            pltpu.VMEM((TRAITS, 8, rows), jnp.float32),
            pltpu.VMEM((STACK, rows), jnp.float32),
            pltpu.VMEM((2 * LANES, rows), jnp.float32),
            pltpu.VMEM((XS, PARTS, LANES), jnp.float32),
            pltpu.VMEM((XS - 1, PARTS, LANES), jnp.float32),
            pltpu.VMEM((zs, PARTS, LANES), jnp.float32),
            pltpu.VMEM((PARTS, LANES), jnp.float32),
            pltpu.VMEM((XS, PARTS, LANES), jnp.float32),
            dma((TRAITS - 1,)),
            dma((TRAITS - 1,)),
            dma((XS - 1,)),
            dma((XS - 1,)),
            dma((zs - 1,)),
            dma((zs - 1,)),
            dma((XS - 1,)),
            dma((XS - 1,)),
        ],
        compiler_params=pltpu.CompilerParams(
            collective_id=2, has_side_effects=True, vmem_limit_bytes=48 << 20
        ),
        name="stack",
    )(genotypes, aux, betas, stats)


def body(genotypes, traits, observed, fold_index):
    local_rows, local_cols = genotypes.shape
    sample_devices = lax.axis_size("samp")
    samples = local_rows * sample_devices
    markers = local_cols * lax.axis_size("blk")
    zs = sample_devices // XS
    aux = jnp.concatenate(
        [
            traits.T,
            observed.T.astype(jnp.float32),
            jnp.broadcast_to(fold_index.astype(jnp.float32)[None], (8, local_rows)),
        ],
        axis=0,
    )
    total = sum_grams(genotypes, aux, zs)
    beta, stats = solve(total, samples, markers)
    betas = share(beta)
    flat = stack(genotypes, aux, betas, stats, zs, FOLDS / samples)
    flat = flat.reshape(XS * PARTS, LANES)
    both = jnp.concatenate([flat[0:STACK], flat[STACK : 2 * STACK]], axis=1)
    end = FOLDS * STACK
    grams = both[:, :end].reshape(STACK, FOLDS, STACK).transpose(1, 2, 0)
    cross = both[:, end : end + FOLDS].T
    return grams[None], cross[None]


def solution(mesh):
    in_specs = (P("samp", "blk"), P("samp", None), P("samp", None), P("samp"))
    out_specs = (P("blk", None, None, None), P("blk", None, None))
    return jax.shard_map(body, mesh=mesh, in_specs=in_specs, out_specs=out_specs, check_vma=False)
```

time: 1170 us -> 133 us (0.11)
  the two profiles are of different devices: /device:TPU:8 before, /device:TPU:4 now
where the time goes in v1:
time: 133 us
  Pallas kernels  126 us (95%)
  local copies, waits for them, and re-layouts  5.27 us (4%)
    pallas_call x1, Pallas kernels, sum_grams(): pl.pallas_call(functools.partial(gram_kernel, zs, chunk), out_shape=jax.S...  57 us
    pallas_call x1, Pallas kernels, stack(): pl.pallas_call(functools.partial(stack_kernel, zs, factor), out_shape=jax...  34.6 us
    pallas_call x1, Pallas kernels, solve(): pl.pallas_call(functools.partial(solve_kernel, samples, markers), out_sha...  25.7 us
    pallas_call x1, Pallas kernels, share(): pl.pallas_call(share_kernel, out_shape=jax.ShapeDtypeStruct((TRAITS, 8, W...  8.95 us
    unnamed x10, local copies, waits for them, and re-layouts  3.86 us

profile of v1, /device:TPU:4, one launch (start us, length us, event | category | flops | bytes accessed | tf_op | source)
XLA Modules:
  0.0 133.0 jit_solution(4814558697160827594)
XLA Ops:
  0.6 0.0 copy-start.2
  0.6 0.7 convert_element_type.11
  1.3 0.0 copy-done.2
  1.4 0.0 copy-start.3
  1.4 0.8 copy-done.3
  2.2 1.5 %copy.7.g_ref = bf16[1024,500]{1,0:T(8,128)(2,1)S(1)} copy(bf16[1024,500]{0,1:T(8,128)(2,1)} %param.4) | data formatting | bytes 2048000 | tf_op args[0]
  3.6 57.0 %sum_grams.1.total_ref = f32[4,344,128]{2,1,0:T(8,128)S(1)} custom-call(bf16[1024,500]{1,0:T(8,128)(2,1)S(1)} %copy.7.g_ref, f32[24,1024]{1,0:T(8,128)S(1)} %pad_maximum_fusion.aux_ref), custom_call_target="tpu_custom_call" | custom-call | tf_op jit(solution)/shard_map/sum_grams/pallas_call | solution.py:225
  60.7 25.7 %solve.1 = (f32[8,512]{1,0:T(8,128)S(1)}, f32[8,128]{1,0:T(8,128)S(1)}) custom-call(f32[4,344,128]{2,1,0:T(8,128)S(1)} %sum_grams.1.total_ref), custom_call_target="tpu_custom_call" | custom-call | tf_op jit(solution)/shard_map/solve/pallas_call | solution.py:401
  86.4 0.0 copy-start.1
  86.4 0.6 copy-done.1
  87.0 8.9 %share.1.beta_ref = f32[8,8,512]{2,1,0:T(8,128)} custom-call(f32[8,512]{1,0:T(8,128)} %copy-done.1), custom_call_target="tpu_custom_call" | custom-call | tf_op jit(solution)/shard_map/share/pallas_call | solution.py:459
  95.9 0.0 copy-start
  96.0 0.9 copy-done
  96.8 34.6 %stack.1 = f32[4,24,128]{2,1,0:T(8,128)S(1)} custom-call(bf16[1024,500]{1,0:T(8,128)(2,1)S(1)} %copy.7.g_ref, f32[24,1024]{1,0:T(8,128)S(1)} %pad_maximum_fusion.aux_ref, f32[8,8,512]{2,1,0:T(8,128)S(1)} %copy-done, f32[8,128]{1,0:T(8,128)S(1)} %get-tuple-element.5.stat_ref), custom_call_target="tpu_custom_call" | custom-call | tf_op jit(solution)/shard_map/stack/pallas_call | solution.py:625
  131.5 0.1 slice.19
  131.6 0.1 copy.10
  131.6 0.6 broadcast_in_dim.14
  132.2 0.7 copy.8
  (5 shorter events, 0.0 us)
Async XLA Ops:
  0.6 0.8 copy-start.2
  1.4 0.8 copy-start.3
  86.4 0.6 copy-start.1
  95.9 0.9 copy-start

commit v2 on v0

v2 whole, which is shorter than its diff:
```python
import functools

import jax
import jax.numpy as jnp
from jax import lax
from jax.experimental import pallas as pl
from jax.experimental.pallas import tpu as pltpu
from jax.sharding import PartitionSpec as P

BLOCK = 500
TRAITS = 8
FOLDS = 5
HERITABILITY = (0.01, 0.25, 0.5, 0.75, 0.99)
PENALTIES = len(HERITABILITY)
PRECISE = lax.Precision.HIGHEST
MESH = pl.DeviceIdType.MESH

XS = 4
LANES = 128
TILES = 4
WIDTH = TILES * LANES
ONES = BLOCK
PAIRS = [(i, j) for i in range(TILES) for j in range(i, TILES)]
EXTRA = 24
FLAT = len(PAIRS) * LANES + TILES * EXTRA
QUARTER = FLAT // XS
ZS = 16
CHUNK = 24
LAYERS = ZS * CHUNK
STACK = PENALTIES * 8
SUMS = 48
PARTS = 2 * SUMS // XS
ORDER = [8, 7, 6, 5, -7, -6, -5, -4, 4, 3, 2, 1, -3, -2, -1, 0]
NEAR = [4, -4, 3, -3, 2, -2, 1, -1]
ARRIVAL = [0, -4, 4, -1, 1, -2, 2, -3, 3, -5, 5, -6, 6, -7, 7, -8]
LAG = 3


def pieces(start, rows):
    out = []
    while rows > 0:
        quarter, row = divmod(start, QUARTER)
        take = min(rows, QUARTER - row)
        out.append((quarter, row, take))
        start += take
        rows -= take
    return out


def put(ref, start, value):
    done = 0
    for quarter, row, take in pieces(start, value.shape[0]):
        ref[quarter, row : row + take, :] = value[done : done + take]
        done += take


def get(ref, start, rows):
    parts = [ref[quarter, row : row + take, :] for quarter, row, take in pieces(start, rows)]
    return parts[0] if len(parts) == 1 else jnp.concatenate(parts, axis=0)


def split3(value):
    first = value.astype(jnp.bfloat16).astype(jnp.float32)
    rest = value - first
    second = rest.astype(jnp.bfloat16).astype(jnp.float32)
    third = rest - second
    return first, second, third


def remote(src, dst, send, recv, samp, blk):
    return pltpu.make_async_remote_copy(
        src_ref=src,
        dst_ref=dst,
        send_sem=send,
        recv_sem=recv,
        device_id=(samp, blk),
        device_id_type=MESH,
    )


def invert(a_ref):
    lane = lax.broadcasted_iota(jnp.int32, (8, LANES), 1)
    sub = lax.broadcasted_iota(jnp.int32, (8, LANES), 0)
    wide = lax.broadcasted_iota(jnp.int32, (LANES, LANES), 1)

    def panel(q, carry):
        base = pl.multiple_of(q * 8, 8)
        shift = lax.rem(LANES - base, LANES)
        strip = a_ref[pl.ds(base, 8), :]
        turned = pltpu.roll(strip, shift, 1)
        cols = [jnp.broadcast_to(turned[:, j : j + 1], (8, LANES)) for j in range(8)]
        inside = jnp.logical_and(lane >= base, lane < base + 8)
        solved = jnp.where(inside, jnp.where(lane - base == sub, -1.0, 0.0), strip)
        for j in range(8):
            inverse = 1.0 / cols[j][j : j + 1, :]
            row = solved[j : j + 1, :] * inverse
            solved = jnp.where(sub == j, row, solved - cols[j] * row)
            for m in range(j + 1, 8):
                value = cols[m][j : j + 1, :] * inverse
                cols[m] = jnp.where(sub == j, value, cols[m] - cols[j] * value)
        whole = a_ref[...]
        turned_all = pltpu.roll(whole, shift, 1)
        within = jnp.logical_and(wide >= base, wide < base + 8)
        result = jnp.where(within, 0.0, whole)
        for j in range(8):
            result = result - turned_all[:, j : j + 1] * solved[j : j + 1, :]
        a_ref[...] = result
        a_ref[pl.ds(base, 8), :] = solved
        return carry

    lax.fori_loop(0, LANES // 8, panel, 0)


def solve_local(samples, markers, place, total_ref, beta_ref, stat_ref, cov, work, inv):
    weight = jnp.float32(0.0)
    for r, fraction in enumerate(HERITABILITY):
        value = jnp.float32(markers * (1.0 - fraction) / fraction)
        chosen = place == r if r < PENALTIES - 1 else place >= r
        weight = jnp.where(chosen, value, weight)

    dot = functools.partial(jnp.dot, precision=PRECISE, preferred_element_type=jnp.float32)

    def dot_t(a, b):
        return lax.dot_general(
            a, b, (((0,), (0,)), ((), ())), precision=PRECISE, preferred_element_type=jnp.float32
        )

    def dot_nt(a, b):
        return lax.dot_general(
            a, b, (((1,), (1,)), ((), ())), precision=PRECISE, preferred_element_type=jnp.float32
        )

    slot = {pair: n for n, pair in enumerate(PAIRS)}
    gram = {pair: get(total_ref, n * LANES, LANES) for pair, n in slot.items()}
    extra = [get(total_ref, len(PAIRS) * LANES + j * EXTRA, EXTRA) for j in range(TILES)]
    eye = lax.broadcasted_iota(jnp.int32, (LANES, LANES), 0) == lax.broadcasted_iota(
        jnp.int32, (LANES, LANES), 1
    )
    mark = ONES - (TILES - 1) * LANES
    sums = extra[-1][0:8, mark : mark + 1]
    counts = extra[-1][8:16, mark : mark + 1]
    squares = extra[-1][16:24, mark + 1 : mark + 2]
    mean_trait = sums / counts
    trait_scale = jnp.sqrt(squares / counts - mean_trait * mean_trait + 1e-05)
    lane8 = lax.broadcasted_iota(jnp.int32, (8, LANES), 1)
    stat_ref[...] = jnp.where(lane8 == 0, mean_trait, jnp.where(lane8 == 1, trait_scale, 0.0))

    sum_row, mean_row, scale_row, sum_col, scale_col = [], [], [], [], []
    for j in range(TILES):
        diagonal = jnp.where(eye, gram[(j, j)], 0.0)
        row = extra[j][16:17, :]
        if j == TILES - 1:
            row = jnp.where(lane8[0:1] < mark, row, 0.0)
        col = gram[(j, TILES - 1)][:, mark : mark + 1]
        mean = row / samples
        mean_c = col / samples
        sum_row.append(row)
        mean_row.append(mean)
        sum_col.append(col)
        squares_row = jnp.sum(diagonal, axis=0, keepdims=True)
        squares_col = jnp.sum(diagonal, axis=1, keepdims=True)
        scale_row.append(jnp.sqrt(squares_row / samples - mean * mean + 1e-05))
        scale_col.append(jnp.sqrt(squares_col / samples - mean_c * mean_c + 1e-05))
    lane = lax.broadcasted_iota(jnp.int32, (LANES, LANES), 1)
    sub = lax.broadcasted_iota(jnp.int32, (LANES, LANES), 0)
    for (i, j), n in slot.items():
        value = (gram[(i, j)] - sum_col[i] * sum_row[j] / samples) / (scale_col[i] * scale_row[j])
        if j == TILES - 1:
            value = jnp.where(lane < mark, value, 0.0)
        if i == TILES - 1:
            value = jnp.where(sub < mark, value, 0.0)
        cov[n] = value
        work[n] = jnp.where(eye, value + weight, value) if i == j else value
    side = []
    for j in range(TILES):
        value = (extra[j][0:8] - extra[j][8:16] * mean_trait) / trait_scale / scale_row[j]
        if j == TILES - 1:
            value = jnp.where(lane8 < mark, value, 0.0)
        side.append(value)

    for k in range(TILES):
        a_ref = inv.at[k]
        a_ref[...] = work[slot[(k, k)]]
        invert(a_ref)
        minus = inv[k]
        for j in range(k + 1, TILES):
            ahead = dot(minus, work[slot[(k, j)]])
            for i in range(k + 1, j + 1):
                n = slot[(i, j)]
                work[n] = work[n] + dot_t(work[slot[(k, i)]], ahead)
        if k < TILES - 1:
            part = dot(side[k], minus)
            for j in range(k + 1, TILES):
                side[j] = side[j] + dot(part, work[slot[(k, j)]])

    found = [None] * TILES
    for k in range(TILES - 1, -1, -1):
        value = side[k]
        for j in range(k + 1, TILES):
            value = value - dot_nt(found[j], work[slot[(k, j)]])
        found[k] = -dot(value, inv[k])

    energy = jnp.zeros((8, 1), jnp.float32)
    shift = jnp.zeros((8, 1), jnp.float32)
    betas = []
    for k in range(TILES):
        image = dot(found[k], cov[slot[(k, k)]])
        for j in range(k + 1, TILES):
            image = image + 2.0 * dot_nt(found[j], cov[slot[(k, j)]])
        energy = energy + jnp.sum(image * found[k], axis=1, keepdims=True)
        beta = found[k] / scale_row[k]
        shift = shift + jnp.sum(beta * mean_row[k], axis=1, keepdims=True)
        betas.append(beta)
    norm = 1.0 / jnp.sqrt(energy / samples + 1e-06)
    for k in range(TILES):
        value = betas[k]
        if k == TILES - 1:
            value = jnp.where(lane8 == mark, -shift, jnp.where(lane8 < mark, value, 0.0))
        beta_ref[:, k * LANES : (k + 1) * LANES] = value * norm


def kernel(
    samples, markers, g_hbm, t_hbm, o_hbm, f_hbm, gram_ref, cross_ref,
    g_ref, t_ref, o_ref, f_ref, last, pay, far_in, fin_l, fin_r, acc, zfar_p, zfar_n, near_in, total,
    cov, work, inv, beta_ref, stat_ref, held, betas, outgoing, incoming, columns, weights, part, x_in,
    z_all, final, in_sem, fs, fr, ls, lr, rs, rr, zs_p, zr_p, zs_n, zr_n, ns, nr, gs, gr, hs_p, hr_p,
    hs_n, hr_n, xls, xlr, xrs, xrr, xfs, xfr, ss, sr, a_send, a_recv, ps, pr, ds, dr, ks_p, kr_p,
    ks_n, kr_n, cs, cr,
):
    samp = lax.axis_index("samp")
    blk = lax.axis_index("blk")
    z = samp // XS
    x = lax.rem(samp, XS)
    right = lax.rem(x + 1, XS)
    left = lax.rem(x + XS - 1, XS)
    far = lax.rem(x + 2, XS)
    group = 2 * XS
    place = lax.rem(samp, group)
    leader = samp - place
    pending = []

    def z_of(d):
        return lax.rem(z + d + ZS, ZS)

    def rows_of(d):
        return pl.ds(pl.multiple_of(z_of(d) * CHUNK, 8), CHUNK)

    def to_z(d, src, dst, send, recv):
        copy = remote(src, dst, send, recv, z_of(d) * XS + x, blk)
        pending.append(copy)
        return copy

    def to_x(there, src, dst, send, recv):
        copy = remote(src, dst, send, recv, z * XS + there, blk)
        pending.append(copy)
        return copy

    loads = [
        pltpu.make_async_copy(src, dst, in_sem.at[i])
        for i, (src, dst) in enumerate(
            [(t_hbm, t_ref), (o_hbm, o_ref), (f_hbm, f_ref), (g_hbm, g_ref)]
        )
    ]
    for load in loads:
        load.start()

    barrier = pltpu.get_barrier_semaphore()
    x_peers = [z * XS + lax.rem(x + i, XS) for i in range(1, XS)]
    z_peers = [z_of(d) * XS + x for d in NEAR]
    twin = leader + XS - (place // XS) * XS
    twins = [twin + lax.rem(x + i, XS) for i in range(1, XS)]
    greeted = x_peers + z_peers + twins
    for other in greeted:
        pl.semaphore_signal(barrier, inc=1, device_id=(other, blk), device_id_type=MESH)
    for i in range(1, TRAITS):
        there = lax.rem(blk + i, TRAITS)
        pl.semaphore_signal(barrier, inc=1, device_id=(samp, there), device_id_type=MESH)

    for load in loads:
        load.wait()
    rows = g_ref.shape[1]
    whole = BLOCK // 16 * 16
    start = (TILES - 1) * LANES
    last[0 : whole - start, :] = g_ref[start:whole, :]
    edge = g_ref[whole:BLOCK, :].astype(jnp.float32)
    sub = lax.broadcasted_iota(jnp.int32, (WIDTH - BLOCK, rows), 0)
    edge = jnp.concatenate([edge, (sub == 0).astype(jnp.float32)], axis=0)
    last[whole - start :, :] = edge.astype(jnp.bfloat16)

    def tile(i):
        return last[...] if i == TILES - 1 else g_ref[i * LANES : (i + 1) * LANES, :]

    nt = (((1,), (1,)), ((), ()))
    traits = t_ref[...]
    present = o_ref[...].astype(jnp.float32)
    masked = traits * present
    squares = jnp.sum(masked * traits, axis=1, keepdims=True)
    ones = (lax.broadcasted_iota(jnp.int32, masked.shape, 0) == 0).astype(jnp.float32)
    stacked = jnp.concatenate([*split3(masked), present, ones], axis=0).astype(jnp.bfloat16)
    slot = 0
    for i in range(TILES):
        for j in range(i, TILES):
            value = lax.dot_general(tile(i), tile(j), nt, preferred_element_type=jnp.float32)
            put(pay, slot * LANES, value)
            slot += 1
    for j in range(TILES):
        cols = lax.dot_general(stacked, tile(j), nt, preferred_element_type=jnp.float32)
        rest = cols[32:40]
        if j == TILES - 1:
            lane = lax.broadcasted_iota(jnp.int32, rest.shape, 1)
            rest = jnp.where(lane == ONES + 1 - j * LANES, squares, rest)
        base = len(PAIRS) * LANES + j * EXTRA
        put(pay, base, cols[0:8] + (cols[8:16] + cols[16:24]))
        put(pay, base + 8, cols[24:32])
        put(pay, base + 16, rest)
    for q in range(XS):
        pay[q, QUARTER:, :] = jnp.zeros((LAYERS - QUARTER, LANES), jnp.float32)

    pl.semaphore_wait(barrier, len(greeted) + TRAITS - 1)

    hop, direct, final_l, final_r = [], [], [], []
    for i, d in enumerate(ORDER):
        here = rows_of(d)
        even_step = i % 2 == 0
        toward, away = (right, left) if even_step else (left, right)
        hop.append(to_x(toward, pay.at[far, here], far_in.at[i], fs.at[i], fr.at[i]))
        goes_r = to_x(right, pay.at[right, here], fin_l.at[i], ls.at[i], lr.at[i])
        goes_l = to_x(left, pay.at[left, here], fin_r.at[i], rs.at[i], rr.at[i])
        final_l.append(goes_r)
        final_r.append(goes_l)

    def first_step(seg):
        for i in range(4 * seg, 4 * seg + 4):
            hop[i].start()
        for i in range(4 * seg, 4 * seg + 4):
            (final_r if i % 2 == 0 else final_l)[i].start()

    def second_step(seg):
        for i in range(4 * seg, 4 * seg + 4):
            here = rows_of(ORDER[i])
            there = right if i % 2 == 0 else left
            hop[i].wait_recv()
            pay[there, here, :] = pay[there, here, :] + far_in[i]
            (final_l if i % 2 == 0 else final_r)[i].start()

    zfar, near = {}, {}
    for i, d in enumerate(ORDER):
        if d > 4:
            zfar[d] = to_z(4, acc.at[i], zfar_p.at[d - 5], zs_p.at[d - 5], zr_p.at[d - 5])
        elif d < -4:
            zfar[d] = to_z(-4, acc.at[i], zfar_n.at[-d - 5], zs_n.at[-d - 5], zr_n.at[-d - 5])
        elif d != 0:
            n = NEAR.index(d)
            near[d] = to_z(d, acc.at[i], near_in.at[n], ns.at[n], nr.at[n])

    def third_step(seg):
        for i in range(4 * seg, 4 * seg + 4):
            d = ORDER[i]
            final_l[i].wait_recv()
            final_r[i].wait_recv()
            value = pay[x, rows_of(d), :] + (fin_l[i] + fin_r[i])
            if 1 <= d <= 4:
                zfar[d + 4].wait_recv()
                value = value + zfar_p[d - 1]
            elif -3 <= d <= -1:
                zfar[d - 4].wait_recv()
                value = value + zfar_n[-d - 1]
            acc[i] = value
            if d in zfar:
                zfar[d].start()
            elif d != 0:
                near[d].start()

    first_step(0)
    first_step(1)
    second_step(0)
    first_step(2)
    second_step(1)
    first_step(3)
    third_step(0)
    second_step(2)
    third_step(1)
    second_step(3)
    third_step(2)
    third_step(3)
    value = acc[ORDER.index(0)]
    for n, d in enumerate(NEAR):
        near[d].wait_recv()
        value = value + near_in[n]
    own = rows_of(0)
    total[x, own, :] = value

    spread = {}
    for n, d in enumerate(NEAR):
        spread[-d] = to_z(d, total.at[x, own], total.at[x, own], gs.at[n], gr.at[n])
        spread[-d].start()
    up, down = rows_of(-4), rows_of(4)
    for e in range(4, 0, -1):
        spread[-4 - e] = to_z(e, total.at[x, up], total.at[x, up], hs_p.at[e - 1], hr_p.at[e - 1])
    for e in range(3, 0, -1):
        spread[4 + e] = to_z(-e, total.at[x, down], total.at[x, down], hs_n.at[e - 1], hr_n.at[e - 1])

    goes_r, goes_l, relay = [], [], []
    for j, o in enumerate(ARRIVAL):
        here = rows_of(o)
        goes_r.append(to_x(right, total.at[x, here], total.at[x, here], xls.at[j], xlr.at[j]))
        goes_l.append(to_x(left, total.at[x, here], total.at[x, here], xrs.at[j], xrr.at[j]))
        toward, origin = (right, left) if j % 2 == 0 else (left, right)
        relay.append(to_x(toward, total.at[origin, here], total.at[origin, here], xfs.at[j], xfr.at[j]))

    def pass_on(j):
        (goes_r if j % 2 == 0 else goes_l)[j].wait_recv()
        relay[j].start()

    for j, o in enumerate(ARRIVAL):
        if o != 0:
            spread[o].wait_recv()
        if o == -4:
            for e in range(4, 0, -1):
                spread[-4 - e].start()
        if o == 4:
            for e in range(3, 0, -1):
                spread[4 + e].start()
        goes_r[j].start()
        goes_l[j].start()
        if j >= LAG:
            pass_on(j - LAG)
    for j in range(ZS - LAG, ZS):
        pass_on(j)
    for j in range(ZS):
        (goes_l if j % 2 == 0 else goes_r)[j].wait_recv()
        relay[j].wait_recv()

    solve_local(samples, markers, place, total, beta_ref, stat_ref, cov, work, inv)

    def give(i):
        other = leader + lax.rem(place + i + 1, group)
        return remote(beta_ref, held.at[place], ss.at[i], sr.at[place], other, blk)

    @pl.when(place < PENALTIES)
    def _():
        for i in range(group - 1):
            give(i).start()
        held[place] = beta_ref[...]

    mean = stat_ref[:, 0:1]
    scale = stat_ref[:, 1:2]
    which = lax.broadcasted_iota(jnp.int32, (8, rows), 0) == blk
    mine = jnp.sum(jnp.where(which, present, 0.0), axis=0, keepdims=True)
    scaled = present * (traits - mean) / scale
    scaled = jnp.sum(jnp.where(which, scaled, 0.0), axis=0, keepdims=True)

    for r in range(PENALTIES):

        @pl.when(place != r)
        def _():
            pltpu.make_async_copy(held.at[r], held.at[r], sr.at[r]).wait()

    betas[...] = jnp.zeros_like(betas)
    for r in range(PENALTIES):
        betas[:, r, :] = held[r]
    n = TRAITS * 8
    beta = betas[...].reshape(n, WIDTH)
    beta = jnp.concatenate(split3(beta), axis=0).astype(jnp.bfloat16)
    predicted = jnp.dot(beta[:, start:], last[...], preferred_element_type=jnp.float32)
    predicted = predicted + jnp.dot(
        beta[:, :start], g_ref[0:start, :], preferred_element_type=jnp.float32
    )
    predicted = predicted[0:n] + (predicted[n : 2 * n] + predicted[2 * n :])
    outgoing[...] = predicted.reshape(TRAITS, 8, rows)

    used = pl.ds(0, PENALTIES)
    exchange = []
    for i in range(TRAITS - 1):
        there = lax.rem(blk + i + 1, TRAITS)
        copy = remote(
            outgoing.at[there, used], incoming.at[blk, used], a_send.at[i], a_recv.at[i], samp, there
        )
        copy.start()
        pending.append(copy)
        exchange.append(copy)
    incoming[blk] = outgoing[blk]
    for copy in exchange:
        copy.wait_recv()

    for b in range(TRAITS):
        columns[b * PENALTIES : (b + 1) * PENALTIES, :] = incoming[b, 0:PENALTIES, :]
    columns[STACK:, :] = jnp.broadcast_to(scaled, (SUMS - STACK, rows))
    level = columns[0:STACK, :]
    fold = f_ref[...]
    for k in range(FOLDS):
        weights[k * STACK : (k + 1) * STACK, :] = level * jnp.where(fold == k, mine, 0.0)
    end = FOLDS * STACK
    weights[end:, :] = jnp.zeros((weights.shape[0] - end, rows), jnp.float32)
    local = lax.dot_general(
        columns[...], weights[...], nt, precision=PRECISE, preferred_element_type=jnp.float32
    )
    flat = jnp.concatenate([local[:, 0:LANES], local[:, LANES:]], axis=0)
    for q in range(XS):
        part[q] = flat[q * PARTS : (q + 1) * PARTS]

    sums = []
    for i in range(XS - 1):
        there = lax.rem(x + i + 1, XS)
        sums.append(to_x(there, part.at[there], x_in.at[i], ps.at[i], pr.at[i]))
        sums[i].start()
    for copy in sums:
        copy.wait_recv()
    z_all[z] = part[x] + (x_in[0] + (x_in[1] + x_in[2]))
    spread = {}
    for n, d in enumerate(NEAR):
        spread[-d] = to_z(d, z_all.at[z], z_all.at[z], ds.at[n], dr.at[n])
        spread[-d].start()
    up, down = z_of(-4), z_of(4)
    for e in range(4, 0, -1):
        spread[-4 - e] = to_z(e, z_all.at[up], z_all.at[up], ks_p.at[e - 1], kr_p.at[e - 1])
    for e in range(3, 0, -1):
        spread[4 + e] = to_z(-e, z_all.at[down], z_all.at[down], ks_n.at[e - 1], kr_n.at[e - 1])
    spread[-4].wait_recv()
    for e in range(4, 0, -1):
        spread[-4 - e].start()
    spread[4].wait_recv()
    for e in range(3, 0, -1):
        spread[4 + e].start()
    for o, copy in spread.items():
        if o not in (4, -4):
            copy.wait_recv()
    value = z_all[0]
    for i in range(1, ZS):
        value = value + z_all[i]
    final[x] = value * (FOLDS / samples)
    collect = []
    for i in range(XS - 1):
        there = lax.rem(x + i + 1, XS)
        collect.append(to_x(there, final.at[x], final.at[x], cs.at[i], cr.at[i]))
        collect[i].start()
    for copy in collect:
        copy.wait_recv()
    low = jnp.concatenate([final[0], final[1]], axis=0)
    high = jnp.concatenate([final[2], final[3]], axis=0)
    both = jnp.concatenate([low, high], axis=1)
    for k in range(FOLDS):
        gram_ref[k] = both[0:STACK, k * STACK : (k + 1) * STACK]
        cross_ref[k : k + 1, :] = both[STACK : STACK + 1, k * STACK : (k + 1) * STACK]

    for copy in pending:
        copy.wait_send()

    @pl.when(place < PENALTIES)
    def _():
        for i in range(group - 1):
            give(i).wait_send()


def body(genotypes, traits, observed, fold_index):
    rows, local_cols = genotypes.shape
    samples = rows * lax.axis_size("samp")
    markers = local_cols * lax.axis_size("blk")
    vmem = pl.BlockSpec(memory_space=pltpu.VMEM)
    hbm = pl.BlockSpec(memory_space=pltpu.MemorySpace.HBM)
    dma = pltpu.SemaphoreType.DMA
    f32 = jnp.float32
    chunks = (ZS, CHUNK, LANES)
    grams, cross = pl.pallas_call(
        functools.partial(kernel, samples, markers),
        out_shape=(
            jax.ShapeDtypeStruct((FOLDS, STACK, STACK), f32),
            jax.ShapeDtypeStruct((FOLDS, STACK), f32),
        ),
        in_specs=[hbm] * 4,
        out_specs=(vmem, vmem),
        scratch_shapes=[
            pltpu.VMEM((BLOCK, rows), jnp.bfloat16),
            pltpu.VMEM((TRAITS, rows), f32),
            pltpu.VMEM((TRAITS, rows), jnp.int32),
            pltpu.VMEM((1, rows), jnp.int32),
            pltpu.VMEM((LANES, rows), jnp.bfloat16),
            pltpu.VMEM((XS, LAYERS, LANES), f32),
            pltpu.VMEM(chunks, f32),
            pltpu.VMEM(chunks, f32),
            pltpu.VMEM(chunks, f32),
            pltpu.VMEM(chunks, f32),
            pltpu.VMEM((4, CHUNK, LANES), f32),
            pltpu.VMEM((3, CHUNK, LANES), f32),
            pltpu.VMEM((8, CHUNK, LANES), f32),
            pltpu.VMEM((XS, LAYERS, LANES), f32),
            pltpu.VMEM((len(PAIRS), LANES, LANES), f32),
            pltpu.VMEM((len(PAIRS), LANES, LANES), f32),
            pltpu.VMEM((TILES, LANES, LANES), f32),
            pltpu.VMEM((8, WIDTH), f32),
            pltpu.VMEM((8, LANES), f32),
            pltpu.VMEM((PENALTIES, 8, WIDTH), f32),
            pltpu.VMEM((TRAITS, 8, WIDTH), f32),
            pltpu.VMEM((TRAITS, 8, rows), f32),
            pltpu.VMEM((TRAITS, 8, rows), f32),
            pltpu.VMEM((SUMS, rows), f32),
            pltpu.VMEM((2 * LANES, rows), f32),
            pltpu.VMEM((XS, PARTS, LANES), f32),
            pltpu.VMEM((XS - 1, PARTS, LANES), f32),
            pltpu.VMEM((ZS, PARTS, LANES), f32),
            pltpu.VMEM((XS, PARTS, LANES), f32),
            dma((4,)),
            *[dma((ZS,)) for _ in range(6)],
            *[dma((4,)) for _ in range(2)],
            *[dma((3,)) for _ in range(2)],
            *[dma((8,)) for _ in range(4)],
            *[dma((4,)) for _ in range(2)],
            *[dma((3,)) for _ in range(2)],
            *[dma((ZS,)) for _ in range(6)],
            dma((2 * XS - 1,)),
            dma((PENALTIES,)),
            *[dma((TRAITS - 1,)) for _ in range(2)],
            *[dma((XS - 1,)) for _ in range(2)],
            *[dma((8,)) for _ in range(2)],
            *[dma((4,)) for _ in range(2)],
            *[dma((3,)) for _ in range(2)],
            *[dma((XS - 1,)) for _ in range(2)],
        ],
        compiler_params=pltpu.CompilerParams(
            collective_id=0, has_side_effects=True, vmem_limit_bytes=48 << 20
        ),
        name="ridge",
    )(genotypes.T, traits.T, observed.T, fold_index.reshape(1, rows))
    return grams[None], cross[None]


def solution(mesh):
    in_specs = (P("samp", "blk"), P("samp", None), P("samp", None), P("samp"))
    out_specs = (P("blk", None, None, None), P("blk", None, None))
    return jax.shard_map(body, mesh=mesh, in_specs=in_specs, out_specs=out_specs, check_vma=False)
```

time: 1170 us -> 113 us (0.10)
  the two profiles are of different devices: /device:TPU:8 before, /device:TPU:2 now
where the time goes in v2:
time: 113 us
  Pallas kernels  108 us (96%)
  local copies, waits for them, and re-layouts  4.64 us (4%)
    pallas_call x1, Pallas kernels, body(): pl.pallas_call(functools.partial(kernel, samples, markers), out_shape=(ja...  108 us
    unnamed x10, local copies, waits for them, and re-layouts  4.64 us

profile of v2, /device:TPU:2, one launch (start us, length us, event | category | flops | bytes accessed | tf_op | source)
XLA Modules:
  0.0 113.0 jit_solution(13675701927855887018)
XLA Ops:
  0.6 0.0 copy-start.3
  0.6 0.7 copy-done.3
  1.3 0.0 copy-start
  1.3 1.2 %copy-done = bf16[1024,500]{0,1:T(8,128)(2,1)S(1)} copy-done((bf16[1024,500]{0,1:T(8,128)(2,1)S(1)}, bf16[1024,500]{0,1:T(8,128)(2,1)}, u32[]{:S(2)}) %copy-start) | copy-done | bytes 1024024
  2.5 0.0 copy-start.1
  2.5 0.8 copy-done.1
  3.3 0.0 copy-start.2
  3.3 0.8 copy-done.2
  4.1 107.7 %ridge.1 = (f32[5,40,40]{2,1,0:T(8,128)S(1)}, f32[5,40]{1,0:T(8,128)S(1)}) custom-call(bf16[500,1024]{1,0:T(8,128)(2,1)S(1)} %bitcast.6, f32[8,1024]{1,0:T(8,128)S(1)} %bitcast.8, s32[8,1024]{1,0:T(8,128)S(1)} %bitcast.9, s32[1,1024]{1,0:T(1,128)S(1)} %bitcast.10), custom_call_target="tpu_custom_call" | custom-call | tf_op jit(solution)/shard_map/ridge/pallas_call | solution.py:564
  111.7 0.6 copy.6
  112.3 0.6 copy.8
Async XLA Ops:
  0.6 0.7 copy-start.3
  1.3 1.2 %copy-start = (bf16[1024,500]{0,1:T(8,128)(2,1)S(1)}, bf16[1024,500]{0,1:T(8,128)(2,1)}, u32[]{:S(2)}) copy-start(bf16[1024,500]{0,1:T(8,128)(2,1)} %param.4) | copy-start | bytes 3072004
  2.5 0.8 copy-start.1
  3.3 0.8 copy-start.2

commit v3 on v2

--- a/solution.py
+++ b/solution.py
@@ -32,8 +32,8 @@
 PARTS = 2 * SUMS // XS
 ORDER = [8, 7, 6, 5, -7, -6, -5, -4, 4, 3, 2, 1, -3, -2, -1, 0]
 NEAR = [4, -4, 3, -3, 2, -2, 1, -1]
-ARRIVAL = [0, -4, 4, -1, 1, -2, 2, -3, 3, -5, 5, -6, 6, -7, 7, -8]
-LAG = 3
+REACH = 8
+SOLVERS = [(3, 0), (3, 1), (3, 2), (3, 3), (4, 1)]
 
 
 def pieces(start, rows):
@@ -91,13 +91,22 @@
         cols = [jnp.broadcast_to(turned[:, j : j + 1], (8, LANES)) for j in range(8)]
         inside = jnp.logical_and(lane >= base, lane < base + 8)
         solved = jnp.where(inside, jnp.where(lane - base == sub, -1.0, 0.0), strip)
-        for j in range(8):
-            inverse = 1.0 / cols[j][j : j + 1, :]
-            row = solved[j : j + 1, :] * inverse
-            solved = jnp.where(sub == j, row, solved - cols[j] * row)
-            for m in range(j + 1, 8):
-                value = cols[m][j : j + 1, :] * inverse
-                cols[m] = jnp.where(sub == j, value, cols[m] - cols[j] * value)
+        for j in range(0, 8, 2):
+            one, two = cols[j], cols[j + 1]
+            a, b = one[j : j + 1, :], two[j : j + 1, :]
+            c, d = one[j + 1 : j + 2, :], two[j + 1 : j + 2, :]
+            inverse = 1.0 / (a * d - b * c)
+            a, b, c, d = d * inverse, b * inverse, c * inverse, a * inverse
+
+            def step(value):
+                top, low = value[j : j + 1, :], value[j + 1 : j + 2, :]
+                top, low = a * top - b * low, d * low - c * top
+                rest = value - one * top - two * low
+                return jnp.where(sub == j, top, jnp.where(sub == j + 1, low, rest))
+
+            solved = step(solved)
+            for m in range(j + 2, 8):
+                cols[m] = step(cols[m])
         whole = a_ref[...]
         turned_all = pltpu.roll(whole, shift, 1)
         within = jnp.logical_and(wide >= base, wide < base + 8)
@@ -111,7 +120,7 @@
     lax.fori_loop(0, LANES // 8, panel, 0)
 
 
-def solve_local(samples, markers, place, total_ref, beta_ref, stat_ref, cov, work, inv):
+def solve_local(samples, markers, place, total_ref, beta_ref, cov, work, inv):
     weight = jnp.float32(0.0)
     for r, fraction in enumerate(HERITABILITY):
         value = jnp.float32(markers * (1.0 - fraction) / fraction)
@@ -143,7 +152,6 @@
     mean_trait = sums / counts
     trait_scale = jnp.sqrt(squares / counts - mean_trait * mean_trait + 1e-05)
     lane8 = lax.broadcasted_iota(jnp.int32, (8, LANES), 1)
-    stat_ref[...] = jnp.where(lane8 == 0, mean_trait, jnp.where(lane8 == 1, trait_scale, 0.0))
 
     sum_row, mean_row, scale_row, sum_col, scale_col = [], [], [], [], []
     for j in range(TILES):
@@ -216,15 +224,18 @@
         value = betas[k]
         if k == TILES - 1:
             value = jnp.where(lane8 == mark, -shift, jnp.where(lane8 < mark, value, 0.0))
-        beta_ref[:, k * LANES : (k + 1) * LANES] = value * norm
+        value = value * norm
+        if k == TILES - 1:
+            value = jnp.where(lane8 == mark + 1, mean_trait, value)
+            value = jnp.where(lane8 == mark + 2, trait_scale, value)
+        beta_ref[:, k * LANES : (k + 1) * LANES] = value
 
 
 def kernel(
     samples, markers, g_hbm, t_hbm, o_hbm, f_hbm, gram_ref, cross_ref,
     g_ref, t_ref, o_ref, f_ref, last, pay, far_in, fin_l, fin_r, acc, zfar_p, zfar_n, near_in, total,
-    cov, work, inv, beta_ref, stat_ref, held, betas, outgoing, incoming, columns, weights, part, x_in,
-    z_all, final, in_sem, fs, fr, ls, lr, rs, rr, zs_p, zr_p, zs_n, zr_n, ns, nr, gs, gr, hs_p, hr_p,
-    hs_n, hr_n, xls, xlr, xrs, xrr, xfs, xfr, ss, sr, a_send, a_recv, ps, pr, ds, dr, ks_p, kr_p,
+    cov, work, inv, beta_ref, held, betas, outgoing, incoming, columns, weights, part, x_in,
+    z_all, final, in_sem, fs, fr, ls, lr, rs, rr, zs_p, zr_p, zs_n, zr_n, ns, nr, gs, gr, ss, sr, a_send, a_recv, ps, pr, ds, dr, ks_p, kr_p,
     ks_n, kr_n, cs, cr,
 ):
     samp = lax.axis_index("samp")
@@ -234,10 +245,16 @@
     right = lax.rem(x + 1, XS)
     left = lax.rem(x + XS - 1, XS)
     far = lax.rem(x + 2, XS)
-    group = 2 * XS
+    pending = []
+    group = REACH * XS
     place = lax.rem(samp, group)
     leader = samp - place
-    pending = []
+    spots = [zo * XS + xo for zo, xo in SOLVERS]
+    solvers = [base + spot for base in range(0, ZS * XS, group) for spot in spots]
+    solving = functools.reduce(jnp.logical_or, [place == spot for spot in spots])
+    penalty = functools.reduce(
+        lambda found, r: jnp.where(place == spots[r], r, found), range(PENALTIES), 0
+    )
 
     def z_of(d):
         return lax.rem(z + d + ZS, ZS)
@@ -267,14 +284,27 @@
     barrier = pltpu.get_barrier_semaphore()
     x_peers = [z * XS + lax.rem(x + i, XS) for i in range(1, XS)]
     z_peers = [z_of(d) * XS + x for d in NEAR]
-    twin = leader + XS - (place // XS) * XS
-    twins = [twin + lax.rem(x + i, XS) for i in range(1, XS)]
-    greeted = x_peers + z_peers + twins
+    greeted = x_peers + z_peers
     for other in greeted:
         pl.semaphore_signal(barrier, inc=1, device_id=(other, blk), device_id_type=MESH)
     for i in range(1, TRAITS):
         there = lax.rem(blk + i, TRAITS)
         pl.semaphore_signal(barrier, inc=1, device_id=(samp, there), device_id_type=MESH)
+
+    for solver in solvers:
+
+        @pl.when(samp != solver)
+        def _():
+            pl.semaphore_signal(barrier, inc=1, device_id=(solver, blk), device_id_type=MESH)
+
+    def greet(i, carry):
+        other = lax.rem(samp + i, ZS * XS)
+        pl.semaphore_signal(barrier, inc=1, device_id=(other, blk), device_id_type=MESH)
+        return carry
+
+    @pl.when(solving)
+    def _():
+        lax.fori_loop(1, ZS * XS, greet, 0)
 
     for load in loads:
         load.wait()
@@ -316,9 +346,18 @@
     for q in range(XS):
         pay[q, QUARTER:, :] = jnp.zeros((LAYERS - QUARTER, LANES), jnp.float32)
 
-    pl.semaphore_wait(barrier, len(greeted) + TRAITS - 1)
-
-    hop, direct, final_l, final_r = [], [], [], []
+    expected = len(greeted) + TRAITS - 1 + len(solvers)
+
+    @pl.when(solving)
+    def _():
+        pl.semaphore_wait(barrier, expected - 1 + ZS * XS - 1)
+
+    @pl.when(jnp.logical_not(solving))
+    def _():
+        pl.semaphore_wait(barrier, expected)
+
+
+    hop, final_l, final_r = [], [], []
     for i, d in enumerate(ORDER):
         here = rows_of(d)
         even_step = i % 2 == 0
@@ -390,72 +429,55 @@
     own = rows_of(0)
     total[x, own, :] = value
 
-    spread = {}
-    for n, d in enumerate(NEAR):
-        spread[-d] = to_z(d, total.at[x, own], total.at[x, own], gs.at[n], gr.at[n])
-        spread[-d].start()
-    up, down = rows_of(-4), rows_of(4)
-    for e in range(4, 0, -1):
-        spread[-4 - e] = to_z(e, total.at[x, up], total.at[x, up], hs_p.at[e - 1], hr_p.at[e - 1])
-    for e in range(3, 0, -1):
-        spread[4 + e] = to_z(-e, total.at[x, down], total.at[x, down], hs_n.at[e - 1], hr_n.at[e - 1])
-
-    goes_r, goes_l, relay = [], [], []
-    for j, o in enumerate(ARRIVAL):
-        here = rows_of(o)
-        goes_r.append(to_x(right, total.at[x, here], total.at[x, here], xls.at[j], xlr.at[j]))
-        goes_l.append(to_x(left, total.at[x, here], total.at[x, here], xrs.at[j], xrr.at[j]))
-        toward, origin = (right, left) if j % 2 == 0 else (left, right)
-        relay.append(to_x(toward, total.at[origin, here], total.at[origin, here], xfs.at[j], xfr.at[j]))
-
-    def pass_on(j):
-        (goes_r if j % 2 == 0 else goes_l)[j].wait_recv()
-        relay[j].start()
-
-    for j, o in enumerate(ARRIVAL):
-        if o != 0:
-            spread[o].wait_recv()
-        if o == -4:
-            for e in range(4, 0, -1):
-                spread[-4 - e].start()
-        if o == 4:
-            for e in range(3, 0, -1):
-                spread[4 + e].start()
-        goes_r[j].start()
-        goes_l[j].start()
-        if j >= LAG:
-            pass_on(j - LAG)
-    for j in range(ZS - LAG, ZS):
-        pass_on(j)
-    for j in range(ZS):
-        (goes_l if j % 2 == 0 else goes_r)[j].wait_recv()
-        relay[j].wait_recv()
-
-    solve_local(samples, markers, place, total, beta_ref, stat_ref, cov, work, inv)
+    def report(n):
+        here = total.at[x, own]
+        return remote(here, here, gs.at[n], gr.at[samp], solvers[n], blk)
+
+    for n, solver in enumerate(solvers):
+
+        @pl.when(samp != solver)
+        def _():
+            report(n).start()
 
     def give(i):
-        other = leader + lax.rem(place + i + 1, group)
-        return remote(beta_ref, held.at[place], ss.at[i], sr.at[place], other, blk)
-
-    @pl.when(place < PENALTIES)
+        other = leader + lax.rem(place + i, group)
+        return remote(beta_ref, held.at[penalty], ss.at[i], sr.at[penalty], other, blk)
+
+    def start_give(i, carry):
+        give(i).start()
+        return carry
+
+    def wait_give(i, carry):
+        give(i).wait_send()
+        return carry
+
+    def hear(i, carry):
+        other = lax.rem(samp + i, ZS * XS)
+        there = pl.ds(pl.multiple_of(other // XS * CHUNK, 8), CHUNK)
+        there = total.at[lax.rem(other, XS), there]
+        pltpu.make_async_copy(there, there, gr.at[other]).wait()
+        return carry
+
+    @pl.when(solving)
     def _():
-        for i in range(group - 1):
-            give(i).start()
-        held[place] = beta_ref[...]
-
-    mean = stat_ref[:, 0:1]
-    scale = stat_ref[:, 1:2]
+        lax.fori_loop(1, ZS * XS, hear, 0)
+        solve_local(samples, markers, penalty, total, beta_ref, cov, work, inv)
+        lax.fori_loop(1, group, start_give, 0)
+        held[penalty] = beta_ref[...]
+
+    for r in range(PENALTIES):
+
+        @pl.when(place != spots[r])
+        def _():
+            pltpu.make_async_copy(held.at[r], held.at[r], sr.at[r]).wait()
+
+    mark = ONES
+    mean = held[0, :, mark + 1 : mark + 2]
+    scale = held[0, :, mark + 2 : mark + 3]
     which = lax.broadcasted_iota(jnp.int32, (8, rows), 0) == blk
     mine = jnp.sum(jnp.where(which, present, 0.0), axis=0, keepdims=True)
     scaled = present * (traits - mean) / scale
     scaled = jnp.sum(jnp.where(which, scaled, 0.0), axis=0, keepdims=True)
-
-    for r in range(PENALTIES):
-
-        @pl.when(place != r)
-        def _():
-            pltpu.make_async_copy(held.at[r], held.at[r], sr.at[r]).wait()
-
     betas[...] = jnp.zeros_like(betas)
     for r in range(PENALTIES):
         betas[:, r, :] = held[r]
@@ -546,10 +568,15 @@
     for copy in pending:
         copy.wait_send()
 
-    @pl.when(place < PENALTIES)
+    for n, solver in enumerate(solvers):
+
+        @pl.when(samp != solver)
+        def _():
+            report(n).wait_send()
+
+    @pl.when(solving)
     def _():
-        for i in range(group - 1):
-            give(i).wait_send()
+        lax.fori_loop(1, group, wait_give, 0)
 
 
 def body(genotypes, traits, observed, fold_index):
@@ -588,7 +615,6 @@
             pltpu.VMEM((len(PAIRS), LANES, LANES), f32),
             pltpu.VMEM((TILES, LANES, LANES), f32),
             pltpu.VMEM((8, WIDTH), f32),
-            pltpu.VMEM((8, LANES), f32),
             pltpu.VMEM((PENALTIES, 8, WIDTH), f32),
             pltpu.VMEM((TRAITS, 8, WIDTH), f32),
             pltpu.VMEM((TRAITS, 8, rows), f32),
@@ -603,11 +629,10 @@
             *[dma((ZS,)) for _ in range(6)],
             *[dma((4,)) for _ in range(2)],
             *[dma((3,)) for _ in range(2)],
-            *[dma((8,)) for _ in range(4)],
-            *[dma((4,)) for _ in range(2)],
-            *[dma((3,)) for _ in range(2)],
-            *[dma((ZS,)) for _ in range(6)],
-            dma((2 * XS - 1,)),
+            *[dma((8,)) for _ in range(2)],
+            dma((ZS // REACH * PENALTIES,)),
+            dma((ZS * XS,)),
+            dma((REACH * XS,)),
             dma((PENALTIES,)),
             *[dma((TRAITS - 1,)) for _ in range(2)],
             *[dma((XS - 1,)) for _ in range(2)],
@@ -617,7 +642,7 @@
             *[dma((XS - 1,)) for _ in range(2)],
         ],
         compiler_params=pltpu.CompilerParams(
-            collective_id=0, has_side_effects=True, vmem_limit_bytes=48 << 20
+            collective_id=0, has_side_effects=True, vmem_limit_bytes=67043328
         ),
         name="ridge",
     )(genotypes.T, traits.T, observed.T, fold_index.reshape(1, rows))

time: 113 us -> 109 us (0.965)
  the two profiles are of different devices: /device:TPU:2 before, /device:TPU:32 now
where the time goes in v3:
time: 109 us
  Pallas kernels  106 us (97%)
  local copies, waits for them, and re-layouts  2.8 us (3%)
    pallas_call x1, Pallas kernels, body(): pl.pallas_call(functools.partial(kernel, samples, markers), out_shape=(ja...  106 us
    unnamed x4, local copies, waits for them, and re-layouts  2.8 us

profile of v3, /device:TPU:32, one launch (start us, length us, event | category | flops | bytes accessed | tf_op | source)
XLA Modules:
  0.0 109.2 jit_solution(11680321164040048623)
XLA Ops:
  0.6 105.7 %ridge.1 = (f32[5,40,40]{2,1,0:T(8,128)}, f32[5,40]{1,0:T(8,128)}) custom-call(bf16[500,1024]{1,0:T(8,128)(2,1)} %bitcast.6, f32[8,1024]{1,0:T(8,128)} %bitcast.8, s32[8,1024]{1,0:T(8,128)} %bitcast.9, s32[1,1024]{1,0:T(1,128)} %bitcast.10), custom_call_target="tpu_custom_call" | custom-call | tf_op jit(solution)/shard_map/ridge/pallas_call | solution.py:591
  106.4 0.0 copy-start
  106.4 0.7 copy-done
  107.0 0.6 copy.6
  107.6 1.5 %copy.8 = f32[1,5,40,40]{3,2,1,0:T(8,128)} copy(f32[1,5,40,40]{3,2,1,0:T(8,128)} %bitcast.7) | data formatting | bytes 64000
Async XLA Ops:
  106.4 0.7 copy-start

commit v4 on v3

--- a/solution.py
+++ b/solution.py
@@ -153,7 +153,7 @@
     trait_scale = jnp.sqrt(squares / counts - mean_trait * mean_trait + 1e-05)
     lane8 = lax.broadcasted_iota(jnp.int32, (8, LANES), 1)
 
-    sum_row, mean_row, scale_row, sum_col, scale_col = [], [], [], [], []
+    sum_row, mean_row, inverse_row, mean_col, inverse_col = [], [], [], [], []
     for j in range(TILES):
         diagonal = jnp.where(eye, gram[(j, j)], 0.0)
         row = extra[j][16:17, :]
@@ -164,15 +164,15 @@
         mean_c = col / samples
         sum_row.append(row)
         mean_row.append(mean)
-        sum_col.append(col)
+        mean_col.append(mean_c)
         squares_row = jnp.sum(diagonal, axis=0, keepdims=True)
         squares_col = jnp.sum(diagonal, axis=1, keepdims=True)
-        scale_row.append(jnp.sqrt(squares_row / samples - mean * mean + 1e-05))
-        scale_col.append(jnp.sqrt(squares_col / samples - mean_c * mean_c + 1e-05))
+        inverse_row.append(1.0 / jnp.sqrt(squares_row / samples - mean * mean + 1e-05))
+        inverse_col.append(1.0 / jnp.sqrt(squares_col / samples - mean_c * mean_c + 1e-05))
     lane = lax.broadcasted_iota(jnp.int32, (LANES, LANES), 1)
     sub = lax.broadcasted_iota(jnp.int32, (LANES, LANES), 0)
     for (i, j), n in slot.items():
-        value = (gram[(i, j)] - sum_col[i] * sum_row[j] / samples) / (scale_col[i] * scale_row[j])
+        value = (gram[(i, j)] - mean_col[i] * sum_row[j]) * inverse_col[i] * inverse_row[j]
         if j == TILES - 1:
             value = jnp.where(lane < mark, value, 0.0)
         if i == TILES - 1:
@@ -181,7 +181,7 @@
         work[n] = jnp.where(eye, value + weight, value) if i == j else value
     side = []
     for j in range(TILES):
-        value = (extra[j][0:8] - extra[j][8:16] * mean_trait) / trait_scale / scale_row[j]
+        value = (extra[j][0:8] - extra[j][8:16] * mean_trait) / trait_scale * inverse_row[j]
         if j == TILES - 1:
             value = jnp.where(lane8 < mark, value, 0.0)
         side.append(value)
@@ -216,7 +216,7 @@
         for j in range(k + 1, TILES):
             image = image + 2.0 * dot_nt(found[j], cov[slot[(k, j)]])
         energy = energy + jnp.sum(image * found[k], axis=1, keepdims=True)
-        beta = found[k] / scale_row[k]
+        beta = found[k] * inverse_row[k]
         shift = shift + jnp.sum(beta * mean_row[k], axis=1, keepdims=True)
         betas.append(beta)
     norm = 1.0 / jnp.sqrt(energy / samples + 1e-06)
@@ -290,21 +290,6 @@
     for i in range(1, TRAITS):
         there = lax.rem(blk + i, TRAITS)
         pl.semaphore_signal(barrier, inc=1, device_id=(samp, there), device_id_type=MESH)
-
-    for solver in solvers:
-
-        @pl.when(samp != solver)
-        def _():
-            pl.semaphore_signal(barrier, inc=1, device_id=(solver, blk), device_id_type=MESH)
-
-    def greet(i, carry):
-        other = lax.rem(samp + i, ZS * XS)
-        pl.semaphore_signal(barrier, inc=1, device_id=(other, blk), device_id_type=MESH)
-        return carry
-
-    @pl.when(solving)
-    def _():
-        lax.fori_loop(1, ZS * XS, greet, 0)
 
     for load in loads:
         load.wait()
@@ -346,16 +331,7 @@
     for q in range(XS):
         pay[q, QUARTER:, :] = jnp.zeros((LAYERS - QUARTER, LANES), jnp.float32)
 
-    expected = len(greeted) + TRAITS - 1 + len(solvers)
-
-    @pl.when(solving)
-    def _():
-        pl.semaphore_wait(barrier, expected - 1 + ZS * XS - 1)
-
-    @pl.when(jnp.logical_not(solving))
-    def _():
-        pl.semaphore_wait(barrier, expected)
-
+    pl.semaphore_wait(barrier, len(greeted) + TRAITS - 1)
 
     hop, final_l, final_r = [], [], []
     for i, d in enumerate(ORDER):

time: 109 us -> 108 us (level)
  the two profiles are of different devices: /device:TPU:32 before, /device:TPU:16 now
where the time goes in v4:
time: 108 us
  Pallas kernels  104 us (96%)
  local copies, waits for them, and re-layouts  2.8 us (3%)
    pallas_call x1, Pallas kernels, body(): pl.pallas_call(functools.partial(kernel, samples, markers), out_shape=(ja...  104 us
    unnamed x4, local copies, waits for them, and re-layouts  2.8 us

profile of v4, /device:TPU:16, one launch (start us, length us, event | category | flops | bytes accessed | tf_op | source)
XLA Modules:
  0.0 107.9 jit_solution(13451506882749991226)
XLA Ops:
  0.6 104.4 %ridge.1 = (f32[5,40,40]{2,1,0:T(8,128)}, f32[5,40]{1,0:T(8,128)}) custom-call(bf16[500,1024]{1,0:T(8,128)(2,1)} %bitcast.6, f32[8,1024]{1,0:T(8,128)} %bitcast.8, s32[8,1024]{1,0:T(8,128)} %bitcast.9, s32[1,1024]{1,0:T(1,128)} %bitcast.10), custom_call_target="tpu_custom_call" | custom-call | tf_op jit(solution)/shard_map/ridge/pallas_call | solution.py:567
  105.1 0.0 copy-start
  105.1 0.7 copy-done
  105.7 0.6 copy.6
  106.3 1.5 %copy.8 = f32[1,5,40,40]{3,2,1,0:T(8,128)} copy(f32[1,5,40,40]{3,2,1,0:T(8,128)} %bitcast.7) | data formatting | bytes 64000
Async XLA Ops:
  105.1 0.7 copy-start

commit v5 on v4

--- a/solution.py
+++ b/solution.py
@@ -82,13 +82,22 @@
     lane = lax.broadcasted_iota(jnp.int32, (8, LANES), 1)
     sub = lax.broadcasted_iota(jnp.int32, (8, LANES), 0)
     wide = lax.broadcasted_iota(jnp.int32, (LANES, LANES), 1)
-
-    def panel(q, carry):
-        base = pl.multiple_of(q * 8, 8)
-        shift = lax.rem(LANES - base, LANES)
-        strip = a_ref[pl.ds(base, 8), :]
-        turned = pltpu.roll(strip, shift, 1)
-        cols = [jnp.broadcast_to(turned[:, j : j + 1], (8, LANES)) for j in range(8)]
+    panels = LANES // 8
+
+    def columns_of(strip, base):
+        turned = pltpu.roll(strip, lax.rem(LANES - base, LANES), 1)
+        return [jnp.broadcast_to(turned[:, j : j + 1], (8, LANES)) for j in range(8)]
+
+    def advance(strip, base, solved):
+        cols = columns_of(strip, base)
+        terms = [cols[j] * solved[j : j + 1, :] for j in range(8)]
+        while len(terms) > 1:
+            terms = [terms[i] + terms[i + 1] for i in range(0, len(terms), 2)]
+        inside = jnp.logical_and(lane >= base, lane < base + 8)
+        return jnp.where(inside, 0.0, strip) - terms[0]
+
+    def pivots(strip, base):
+        cols = columns_of(strip, base)
         inside = jnp.logical_and(lane >= base, lane < base + 8)
         solved = jnp.where(inside, jnp.where(lane - base == sub, -1.0, 0.0), strip)
         for j in range(0, 8, 2):
@@ -107,17 +116,35 @@
             solved = step(solved)
             for m in range(j + 2, 8):
                 cols[m] = step(cols[m])
-        whole = a_ref[...]
-        turned_all = pltpu.roll(whole, shift, 1)
+        return solved
+
+    def update(base, strip, solved, keep):
+        a1, a2, a3 = split3(strip)
+        b1, b2, b3 = split3(solved)
+        lhs = jnp.concatenate([a1, a1, a2, a1, a3, a2], axis=0).astype(jnp.bfloat16)
+        rhs = jnp.concatenate([b1, b2, b1, b3, b1, b2], axis=0).astype(jnp.bfloat16)
+        product = lax.dot_general(
+            lhs, rhs, (((0,), (0,)), ((), ())), preferred_element_type=jnp.float32
+        )
         within = jnp.logical_and(wide >= base, wide < base + 8)
-        result = jnp.where(within, 0.0, whole)
-        for j in range(8):
-            result = result - turned_all[:, j : j + 1] * solved[j : j + 1, :]
-        a_ref[...] = result
-        a_ref[pl.ds(base, 8), :] = solved
-        return carry
-
-    lax.fori_loop(0, LANES // 8, panel, 0)
+        a_ref[...] = jnp.where(within, 0.0, a_ref[...]) - product
+        a_ref[pl.ds(pl.multiple_of(jnp.maximum(base, 0), 8), 8), :] = keep
+
+    def panel(q, carry):
+        strip, before, done = carry
+        base = pl.multiple_of(q * 8, 8)
+        ahead = pl.multiple_of(lax.rem(q + 1, panels) * 8, 8)
+        coming = a_ref[pl.ds(ahead, 8), :]
+        last = lax.rem(base - 8 + LANES, LANES)
+        moved = advance(coming, last, done)
+        coming = jnp.where(q > 0, moved, coming)
+        solved = pivots(strip, base)
+        update(base - 8, before, done, jnp.where(q > 0, done, strip))
+        return advance(coming, base, solved), strip, solved
+
+    zero = jnp.zeros((8, LANES), jnp.float32)
+    strip, before, done = lax.fori_loop(0, panels, panel, (a_ref[0:8, :], zero, zero))
+    update(LANES - 8, before, done, done)
 
 
 def solve_local(samples, markers, place, total_ref, beta_ref, cov, work, inv):

time: 108 us -> 110 us (1.019)
  Pallas kernels: 104 us -> 106 us
    pallas_call x1, Pallas kernels: 104 us -> 106 us  [body(): pl.pallas_call(functools.partial(kernel, samples, markers), out_shape=(ja...]
where the time goes in v5:
time: 110 us; the launch traced here: 109 us
  Pallas kernels  106 us (96%)
  local copies, waits for them, and re-layouts  2.8 us (3%)
    pallas_call x1, Pallas kernels, body(): pl.pallas_call(functools.partial(kernel, samples, markers), out_shape=(ja...  106 us
    unnamed x4, local copies, waits for them, and re-layouts  2.8 us

profile of v5, /device:TPU:16, one launch (start us, length us, event | category | flops | bytes accessed | tf_op | source)
XLA Modules:
  0.0 109.5 jit_solution(16833294180049472946)
XLA Ops:
  0.6 106.0 %ridge.1 = (f32[5,40,40]{2,1,0:T(8,128)}, f32[5,40]{1,0:T(8,128)}) custom-call(bf16[500,1024]{1,0:T(8,128)(2,1)} %bitcast.6, f32[8,1024]{1,0:T(8,128)} %bitcast.8, s32[8,1024]{1,0:T(8,128)} %bitcast.9, s32[1,1024]{1,0:T(1,128)} %bitcast.10), custom_call_target="tpu_custom_call" | custom-call | tf_op jit(solution)/shard_map/ridge/pallas_call | solution.py:594
  106.7 0.0 copy-start
  106.7 0.7 copy-done
  107.4 0.6 copy.6
  107.9 1.5 %copy.8 = f32[1,5,40,40]{3,2,1,0:T(8,128)} copy(f32[1,5,40,40]{3,2,1,0:T(8,128)} %bitcast.7) | data formatting | bytes 64000
Async XLA Ops:
  106.7 0.7 copy-start

commit v6 on v5

--- a/solution.py
+++ b/solution.py
@@ -82,11 +82,9 @@
     lane = lax.broadcasted_iota(jnp.int32, (8, LANES), 1)
     sub = lax.broadcasted_iota(jnp.int32, (8, LANES), 0)
     wide = lax.broadcasted_iota(jnp.int32, (LANES, LANES), 1)
-    panels = LANES // 8
 
     def columns_of(strip, base):
-        turned = pltpu.roll(strip, lax.rem(LANES - base, LANES), 1)
-        return [jnp.broadcast_to(turned[:, j : j + 1], (8, LANES)) for j in range(8)]
+        return [jnp.broadcast_to(strip[:, base + j : base + j + 1], (8, LANES)) for j in range(8)]
 
     def advance(strip, base, solved):
         cols = columns_of(strip, base)
@@ -118,7 +116,7 @@
                 cols[m] = step(cols[m])
         return solved
 
-    def update(base, strip, solved, keep):
+    def update(base, strip, solved):
         a1, a2, a3 = split3(strip)
         b1, b2, b3 = split3(solved)
         lhs = jnp.concatenate([a1, a1, a2, a1, a3, a2], axis=0).astype(jnp.bfloat16)
@@ -128,23 +126,21 @@
         )
         within = jnp.logical_and(wide >= base, wide < base + 8)
         a_ref[...] = jnp.where(within, 0.0, a_ref[...]) - product
-        a_ref[pl.ds(pl.multiple_of(jnp.maximum(base, 0), 8), 8), :] = keep
-
-    def panel(q, carry):
-        strip, before, done = carry
-        base = pl.multiple_of(q * 8, 8)
-        ahead = pl.multiple_of(lax.rem(q + 1, panels) * 8, 8)
-        coming = a_ref[pl.ds(ahead, 8), :]
-        last = lax.rem(base - 8 + LANES, LANES)
-        moved = advance(coming, last, done)
-        coming = jnp.where(q > 0, moved, coming)
+        a_ref[base : base + 8, :] = solved
+
+    strip = a_ref[0:8, :]
+    before = done = None
+    for base in range(0, LANES, 8):
+        ahead = (base + 8) % LANES
+        coming = a_ref[ahead : ahead + 8, :]
+        if base > 0:
+            coming = advance(coming, base - 8, done)
         solved = pivots(strip, base)
-        update(base - 8, before, done, jnp.where(q > 0, done, strip))
-        return advance(coming, base, solved), strip, solved
-
-    zero = jnp.zeros((8, LANES), jnp.float32)
-    strip, before, done = lax.fori_loop(0, panels, panel, (a_ref[0:8, :], zero, zero))
-    update(LANES - 8, before, done, done)
+        if base > 0:
+            update(base - 8, before, done)
+        before, done = strip, solved
+        strip = advance(coming, base, solved)
+    update(LANES - 8, before, done)
 
 
 def solve_local(samples, markers, place, total_ref, beta_ref, cov, work, inv):

time: 110 us -> 102 us (0.927)
  Pallas kernels: 106 us -> 98.3 us
    pallas_call x1, Pallas kernels: 106 us -> 98.3 us  [body(): pl.pallas_call(functools.partial(kernel, samples, markers), out_shape=(ja...]
where the time goes in v6:
time: 102 us
  Pallas kernels  98.3 us (96%)
  local copies, waits for them, and re-layouts  2.8 us (3%)
    pallas_call x1, Pallas kernels, body(): pl.pallas_call(functools.partial(kernel, samples, markers), out_shape=(ja...  98.3 us
    unnamed x4, local copies, waits for them, and re-layouts  2.8 us

profile of v6, /device:TPU:16, one launch (start us, length us, event | category | flops | bytes accessed | tf_op | source)
XLA Modules:
  0.0 101.7 jit_solution(1065776626247998780)
XLA Ops:
  0.6 98.3 %ridge.1 = (f32[5,40,40]{2,1,0:T(8,128)}, f32[5,40]{1,0:T(8,128)}) custom-call(bf16[500,1024]{1,0:T(8,128)(2,1)} %bitcast.6, f32[8,1024]{1,0:T(8,128)} %bitcast.8, s32[8,1024]{1,0:T(8,128)} %bitcast.9, s32[1,1024]{1,0:T(1,128)} %bitcast.10), custom_call_target="tpu_custom_call" | custom-call | tf_op jit(solution)/shard_map/ridge/pallas_call | solution.py:590
  98.9 0.0 copy-start
  98.9 0.7 copy-done
  99.6 0.6 copy.6
  100.2 1.5 %copy.8 = f32[1,5,40,40]{3,2,1,0:T(8,128)} copy(f32[1,5,40,40]{3,2,1,0:T(8,128)} %bitcast.7) | data formatting | bytes 64000
Async XLA Ops:
  98.9 0.7 copy-start
